TPU v7x, 128 devices: a whole 4x4x4 slice. The times are simulated.
128 devices in a mesh: ctx: 16 (over x, z_lo, core), heads: 8 (over z_hi, y).
Axes of the slice: x: 4, y: 4, z: 4 (z_hi: 2, z_lo: 2; z = z_hi * 2 + z_lo), core: 2. Of those that a mesh axis runs over, the one named last changes fastest.
Arguments:
- queries: bfloat16 [1024, 16384], P('ctx', 'heads'), may hold values from -40 to 40
- cache_keys: bfloat16 [2, 32768, 1024], P(None, 'ctx', 'heads'), may hold values from -10 to 10
- cache_values: bfloat16 [2, 32768, 1024], P(None, 'ctx', 'heads'), may hold values from -6 to 6
- bounds: int32 [2, 2], replicated, may hold values from 1 to 32768, as said below
- out_weight: bfloat16 [16384, 16384], P('heads', 'ctx'), may hold values from -0.046875 to 0.046875
- residual: bfloat16 [1024, 16384], P('heads', 'ctx'), may hold values from -3 to 3
Outputs:
- layer_out: bfloat16 [1024, 16384], P('heads', 'ctx')
Inputs may be any that keep to these rules, and one draw needn't show every extreme that they name: bounds[p, 0] lies between 16384 and 32256; bounds[p, 1] - bounds[p, 0] lies between 1 and 512.
All inputs are finite; a program needn't handle non-finite values.
Results may differ from a plain program's by a relative error of at most 0.012.
Values may be sent and summed in bfloat16 or wider, within the bound.
A program may use at most 64 MiB of HBM per device.

v0:
```python
import math

import jax
import jax.numpy as jnp
from jax import lax
from jax.sharding import PartitionSpec as P

H = 128
KV = 8
HD = 128
Q = 512


NEG_FILL = -1e30


def shifted(block, axis, distance):
    devices = range(lax.axis_size(axis))
    route = [((i - distance) % len(devices), i) for i in devices]
    return lax.ppermute(block, axis, route)


def empty_state(rows, local_kv, groups):
    running_max = jnp.full((rows, local_kv, groups), NEG_FILL, jnp.float32)
    weight_sum = jnp.zeros((rows, local_kv, groups), jnp.float32)
    numerator = jnp.zeros((rows, local_kv, groups, HD), jnp.float32)
    return (running_max, weight_sum, numerator)


def attend_rows(query_rows, first_row, cache_keys, cache_values, bounds, key_base, state):
    rows = query_rows.shape[0]
    local_kv = cache_keys.shape[2] // HD
    groups = H // KV
    scaling = 1.0 / math.sqrt(HD)
    prompt = first_row // Q
    within = first_row % Q
    limits = lax.dynamic_index_in_dim(bounds, prompt, 0, False)
    query_pos = limits[0] + within + jnp.arange(rows, dtype=jnp.int32)
    keys_here = lax.dynamic_index_in_dim(cache_keys, prompt, 0, False)
    values_here = lax.dynamic_index_in_dim(cache_values, prompt, 0, False)
    span = keys_here.shape[0]
    width = min(512, span)
    shaped_query = query_rows.reshape(rows, local_kv, groups, HD)

    def one_block(block_index, carried):
        running_max, weight_sum, numerator = carried
        key_block = lax.dynamic_slice_in_dim(keys_here, block_index * width, width, 0).reshape(
            width, local_kv, HD
        )
        value_block = lax.dynamic_slice_in_dim(values_here, block_index * width, width, 0).reshape(
            width, local_kv, HD
        )
        key_pos = key_base + block_index * width + jnp.arange(width, dtype=jnp.int32)
        visible = (key_pos[None, :] <= query_pos[:, None]) & (key_pos[None, :] < limits[1])
        visible = visible[:, None, None, :]
        scores = (
            jnp.einsum(
                "rkgd,jkd->rkgj", shaped_query, key_block, preferred_element_type=jnp.float32
            )
            * scaling
        )
        scores = jnp.where(visible, scores, NEG_FILL)
        new_max = jnp.maximum(running_max, jnp.max(scores, axis=3))
        weights = jnp.where(visible, jnp.exp(scores - new_max[..., None]), 0.0)
        keeping = jnp.exp(running_max - new_max)
        weight_sum = weight_sum * keeping + jnp.sum(weights, axis=3)
        numerator = numerator * keeping[..., None] + jnp.einsum(
            "rkgj,jkd->rkgd",
            weights.astype(jnp.bfloat16),
            value_block,
            preferred_element_type=jnp.float32,
        )
        return (new_max, weight_sum, numerator)

    return lax.fori_loop(0, span // width, one_block, state)


def shards(queries, cache_keys, cache_values, bounds, out_weight, residual):
    rows = queries.shape[0]
    local_kv = cache_keys.shape[2] // HD
    groups = H // KV
    cycle_size = lax.axis_size("ctx")
    position = lax.axis_index("ctx")
    key_base = position * cache_keys.shape[1]

    def one_turn(turn_index, carried):
        travelling, running_max, weight_sum, numerator = carried
        owner = (position - turn_index) % cycle_size
        running_max, weight_sum, numerator = attend_rows(
            travelling,
            owner * rows,
            cache_keys,
            cache_values,
            bounds,
            key_base,
            (running_max, weight_sum, numerator),
        )
        return (
            shifted(travelling, "ctx", 1),
            shifted(running_max.astype(jnp.bfloat16), "ctx", 1).astype(running_max.dtype),
            shifted(weight_sum.astype(jnp.bfloat16), "ctx", 1).astype(weight_sum.dtype),
            shifted(numerator.astype(jnp.bfloat16), "ctx", 1).astype(numerator.dtype),
        )

    initial = (queries,) + empty_state(rows, local_kv, groups)
    finished = lax.fori_loop(0, cycle_size, one_turn, initial)
    weight_sum = finished[2]
    numerator = finished[3]
    attended = (
        (numerator / weight_sum[..., None])
        .reshape(rows, local_kv * groups * HD)
        .astype(jnp.bfloat16)
    )
    partial_rows = jnp.dot(
        lax.all_gather(attended, "ctx", axis=0, tiled=True),
        out_weight,
        preferred_element_type=jnp.float32,
    )
    summed = lax.psum_scatter(
        partial_rows.astype(jnp.bfloat16), "heads", scatter_dimension=0, tiled=True
    ).astype(jnp.float32)
    return (residual.astype(jnp.float32) + summed).astype(jnp.bfloat16)


def solution(mesh):
    in_specs = (
        P("ctx", "heads"),
        P(None, "ctx", "heads"),
        P(None, "ctx", "heads"),
        P(),
        P("heads", "ctx"),
        P("heads", "ctx"),
    )
    out_specs = P("heads", "ctx")
    return jax.shard_map(shards, mesh=mesh, in_specs=in_specs, out_specs=out_specs, check_vma=False)
```

profile of v0, /device:TPU:0, one launch (start us, length us, event | category | flops | bytes accessed | tf_op | source)
XLA Modules:
  0.0 580.2 jit_solution(11833562480238718706)
XLA Ops:
  7.5 439.4 %while.83 = (s32[]{:T(128)}, bf16[64,2048]{1,0:T(8,128)(2,1)S(1)}, f32[64,1,16]{0,2,1:T(8,128)S(1)}, f32[64,1,16]{0,2,1:T(8,128)S(1)}, f32[64,1,16,128]{3,0,2,1:...) while((s32[]{:T(128)}, bf16[64,2048]{1,0:T(8,128)(2,1)S(1)}, ...), condition=%wide.region_5.6_spmd.clone, body=%wide.region_0.5_spmd.clone.sunk | while | flops 275982944 | bytes 20716172 | solution.py:106
  10.3 13.6 %while.84 = (s32[]{:T(128)}, f32[64,1,16]{0,2,1:T(8,128)S(1)}, f32[64,1,16]{0,2,1:T(8,128)S(1)}, f32[64,1,16,128]{3,0,2,1:T(8,128)S(1)}, s32[]{:T(128)}, /*index...) while((s32[]{:T(128)}, f32[64,1,16]{0,2,1:T(8,128)S(1)}, ...), condition=%wide.region_4.4_spmd.clone, body=%wide.region_1.3_spmd.clone.sunk | while | flops 275583552 | bytes 8074975 | solution.py:75
  37.8 13.6 %while.84 = (s32[]{:T(128)}, f32[64,1,16]{0,2,1:T(8,128)S(1)}, f32[64,1,16]{0,2,1:T(8,128)S(1)}, f32[64,1,16,128]{3,0,2,1:T(8,128)S(1)}, s32[]{:T(128)}, /*index...) while((s32[]{:T(128)}, f32[64,1,16]{0,2,1:T(8,128)S(1)}, ...), condition=%wide.region_4.4_spmd.clone, body=%wide.region_1.3_spmd.clone.sunk | while | flops 275583552 | bytes 8074975 | solution.py:75
  65.3 13.6 %while.84 = (s32[]{:T(128)}, f32[64,1,16]{0,2,1:T(8,128)S(1)}, f32[64,1,16]{0,2,1:T(8,128)S(1)}, f32[64,1,16,128]{3,0,2,1:T(8,128)S(1)}, s32[]{:T(128)}, /*index...) while((s32[]{:T(128)}, f32[64,1,16]{0,2,1:T(8,128)S(1)}, ...), condition=%wide.region_4.4_spmd.clone, body=%wide.region_1.3_spmd.clone.sunk | while | flops 275583552 | bytes 8074975 | solution.py:75
  92.7 13.6 %while.84 = (s32[]{:T(128)}, f32[64,1,16]{0,2,1:T(8,128)S(1)}, f32[64,1,16]{0,2,1:T(8,128)S(1)}, f32[64,1,16,128]{3,0,2,1:T(8,128)S(1)}, s32[]{:T(128)}, /*index...) while((s32[]{:T(128)}, f32[64,1,16]{0,2,1:T(8,128)S(1)}, ...), condition=%wide.region_4.4_spmd.clone, body=%wide.region_1.3_spmd.clone.sunk | while | flops 275583552 | bytes 8074975 | solution.py:75
  106.7 10.5 %collective-permute-done.2 = bf16[64,1,16]{0,2,1:T(8,128)(2,1)S(1)} collective-permute-done((bf16[64,1,16]{0,2,1:T(8,128)(2,1)S(1)}, bf16[64,1,16]{0,2,1:T(8,128)(2,1)S(1)}, u32[]{:S(2)}, u32[]{:S(2)}) %collective-permute-start.2) | collective-permute-done | bytes 2080 | tf_op jit(solution)/shard_map/while/body/eval_jaxpr/ppermute | solution.py:20
  120.2 13.6 %while.84 = (s32[]{:T(128)}, f32[64,1,16]{0,2,1:T(8,128)S(1)}, f32[64,1,16]{0,2,1:T(8,128)S(1)}, f32[64,1,16,128]{3,0,2,1:T(8,128)S(1)}, s32[]{:T(128)}, /*index...) while((s32[]{:T(128)}, f32[64,1,16]{0,2,1:T(8,128)S(1)}, ...), condition=%wide.region_4.4_spmd.clone, body=%wide.region_1.3_spmd.clone.sunk | while | flops 275583552 | bytes 8074975 | solution.py:75
  134.2 10.5 %collective-permute-done.2 = bf16[64,1,16]{0,2,1:T(8,128)(2,1)S(1)} collective-permute-done((bf16[64,1,16]{0,2,1:T(8,128)(2,1)S(1)}, bf16[64,1,16]{0,2,1:T(8,128)(2,1)S(1)}, u32[]{:S(2)}, u32[]{:S(2)}) %collective-permute-start.2) | collective-permute-done | bytes 2080 | tf_op jit(solution)/shard_map/while/body/eval_jaxpr/ppermute | solution.py:20
  147.7 13.6 %while.84 = (s32[]{:T(128)}, f32[64,1,16]{0,2,1:T(8,128)S(1)}, f32[64,1,16]{0,2,1:T(8,128)S(1)}, f32[64,1,16,128]{3,0,2,1:T(8,128)S(1)}, s32[]{:T(128)}, /*index...) while((s32[]{:T(128)}, f32[64,1,16]{0,2,1:T(8,128)S(1)}, ...), condition=%wide.region_4.4_spmd.clone, body=%wide.region_1.3_spmd.clone.sunk | while | flops 275583552 | bytes 8074975 | solution.py:75
  161.7 10.5 %collective-permute-done.2 = bf16[64,1,16]{0,2,1:T(8,128)(2,1)S(1)} collective-permute-done((bf16[64,1,16]{0,2,1:T(8,128)(2,1)S(1)}, bf16[64,1,16]{0,2,1:T(8,128)(2,1)S(1)}, u32[]{:S(2)}, u32[]{:S(2)}) %collective-permute-start.2) | collective-permute-done | bytes 2080 | tf_op jit(solution)/shard_map/while/body/eval_jaxpr/ppermute | solution.py:20
  175.1 13.6 %while.84 = (s32[]{:T(128)}, f32[64,1,16]{0,2,1:T(8,128)S(1)}, f32[64,1,16]{0,2,1:T(8,128)S(1)}, f32[64,1,16,128]{3,0,2,1:T(8,128)S(1)}, s32[]{:T(128)}, /*index...) while((s32[]{:T(128)}, f32[64,1,16]{0,2,1:T(8,128)S(1)}, ...), condition=%wide.region_4.4_spmd.clone, body=%wide.region_1.3_spmd.clone.sunk | while | flops 275583552 | bytes 8074975 | solution.py:75
  189.1 10.5 %collective-permute-done.2 = bf16[64,1,16]{0,2,1:T(8,128)(2,1)S(1)} collective-permute-done((bf16[64,1,16]{0,2,1:T(8,128)(2,1)S(1)}, bf16[64,1,16]{0,2,1:T(8,128)(2,1)S(1)}, u32[]{:S(2)}, u32[]{:S(2)}) %collective-permute-start.2) | collective-permute-done | bytes 2080 | tf_op jit(solution)/shard_map/while/body/eval_jaxpr/ppermute | solution.py:20
  202.6 13.6 %while.84 = (s32[]{:T(128)}, f32[64,1,16]{0,2,1:T(8,128)S(1)}, f32[64,1,16]{0,2,1:T(8,128)S(1)}, f32[64,1,16,128]{3,0,2,1:T(8,128)S(1)}, s32[]{:T(128)}, /*index...) while((s32[]{:T(128)}, f32[64,1,16]{0,2,1:T(8,128)S(1)}, ...), condition=%wide.region_4.4_spmd.clone, body=%wide.region_1.3_spmd.clone.sunk | while | flops 275583552 | bytes 8074975 | solution.py:75
  216.6 10.5 %collective-permute-done.2 = bf16[64,1,16]{0,2,1:T(8,128)(2,1)S(1)} collective-permute-done((bf16[64,1,16]{0,2,1:T(8,128)(2,1)S(1)}, bf16[64,1,16]{0,2,1:T(8,128)(2,1)S(1)}, u32[]{:S(2)}, u32[]{:S(2)}) %collective-permute-start.2) | collective-permute-done | bytes 2080 | tf_op jit(solution)/shard_map/while/body/eval_jaxpr/ppermute | solution.py:20
  230.1 13.6 %while.84 = (s32[]{:T(128)}, f32[64,1,16]{0,2,1:T(8,128)S(1)}, f32[64,1,16]{0,2,1:T(8,128)S(1)}, f32[64,1,16,128]{3,0,2,1:T(8,128)S(1)}, s32[]{:T(128)}, /*index...) while((s32[]{:T(128)}, f32[64,1,16]{0,2,1:T(8,128)S(1)}, ...), condition=%wide.region_4.4_spmd.clone, body=%wide.region_1.3_spmd.clone.sunk | while | flops 275583552 | bytes 8074975 | solution.py:75
  257.6 13.6 %while.84 = (s32[]{:T(128)}, f32[64,1,16]{0,2,1:T(8,128)S(1)}, f32[64,1,16]{0,2,1:T(8,128)S(1)}, f32[64,1,16,128]{3,0,2,1:T(8,128)S(1)}, s32[]{:T(128)}, /*index...) while((s32[]{:T(128)}, f32[64,1,16]{0,2,1:T(8,128)S(1)}, ...), condition=%wide.region_4.4_spmd.clone, body=%wide.region_1.3_spmd.clone.sunk | while | flops 275583552 | bytes 8074975 | solution.py:75
  285.0 13.6 %while.84 = (s32[]{:T(128)}, f32[64,1,16]{0,2,1:T(8,128)S(1)}, f32[64,1,16]{0,2,1:T(8,128)S(1)}, f32[64,1,16,128]{3,0,2,1:T(8,128)S(1)}, s32[]{:T(128)}, /*index...) while((s32[]{:T(128)}, f32[64,1,16]{0,2,1:T(8,128)S(1)}, ...), condition=%wide.region_4.4_spmd.clone, body=%wide.region_1.3_spmd.clone.sunk | while | flops 275583552 | bytes 8074975 | solution.py:75
  312.5 13.6 %while.84 = (s32[]{:T(128)}, f32[64,1,16]{0,2,1:T(8,128)S(1)}, f32[64,1,16]{0,2,1:T(8,128)S(1)}, f32[64,1,16,128]{3,0,2,1:T(8,128)S(1)}, s32[]{:T(128)}, /*index...) while((s32[]{:T(128)}, f32[64,1,16]{0,2,1:T(8,128)S(1)}, ...), condition=%wide.region_4.4_spmd.clone, body=%wide.region_1.3_spmd.clone.sunk | while | flops 275583552 | bytes 8074975 | solution.py:75
  340.0 13.6 %while.84 = (s32[]{:T(128)}, f32[64,1,16]{0,2,1:T(8,128)S(1)}, f32[64,1,16]{0,2,1:T(8,128)S(1)}, f32[64,1,16,128]{3,0,2,1:T(8,128)S(1)}, s32[]{:T(128)}, /*index...) while((s32[]{:T(128)}, f32[64,1,16]{0,2,1:T(8,128)S(1)}, ...), condition=%wide.region_4.4_spmd.clone, body=%wide.region_1.3_spmd.clone.sunk | while | flops 275583552 | bytes 8074975 | solution.py:75
  367.4 13.6 %while.84 = (s32[]{:T(128)}, f32[64,1,16]{0,2,1:T(8,128)S(1)}, f32[64,1,16]{0,2,1:T(8,128)S(1)}, f32[64,1,16,128]{3,0,2,1:T(8,128)S(1)}, s32[]{:T(128)}, /*index...) while((s32[]{:T(128)}, f32[64,1,16]{0,2,1:T(8,128)S(1)}, ...), condition=%wide.region_4.4_spmd.clone, body=%wide.region_1.3_spmd.clone.sunk | while | flops 275583552 | bytes 8074975 | solution.py:75
  394.9 13.6 %while.84 = (s32[]{:T(128)}, f32[64,1,16]{0,2,1:T(8,128)S(1)}, f32[64,1,16]{0,2,1:T(8,128)S(1)}, f32[64,1,16,128]{3,0,2,1:T(8,128)S(1)}, s32[]{:T(128)}, /*index...) while((s32[]{:T(128)}, f32[64,1,16]{0,2,1:T(8,128)S(1)}, ...), condition=%wide.region_4.4_spmd.clone, body=%wide.region_1.3_spmd.clone.sunk | while | flops 275583552 | bytes 8074975 | solution.py:75
  422.4 13.6 %while.84 = (s32[]{:T(128)}, f32[64,1,16]{0,2,1:T(8,128)S(1)}, f32[64,1,16]{0,2,1:T(8,128)S(1)}, f32[64,1,16,128]{3,0,2,1:T(8,128)S(1)}, s32[]{:T(128)}, /*index...) while((s32[]{:T(128)}, f32[64,1,16]{0,2,1:T(8,128)S(1)}, ...), condition=%wide.region_4.4_spmd.clone, body=%wide.region_1.3_spmd.clone.sunk | while | flops 275583552 | bytes 8074975 | solution.py:75
  448.2 37.2 %all-gather.2.cloned.1.call-done = bf16[1024,2048]{1,0:T(8,128)(2,1)} async-done(((bf16[64,2048]{1,0:T(8,128)(2,1)}), bf16[1024,2048]{1,0:T(8,128)(2,1)}) %all-gather.2.cloned.1.call-update) | async-done | bytes 4194320 | tf_op jit(solution)/shard_map/all_gather | solution.py:115
  494.7 76.9 %reduce-scatter.2.cloned.1.call-done = bf16[128,1024]{1,0:T(8,128)(2,1)} async-done(((bf16[1024,1024]{1,0:T(8,128)(2,1)}), bf16[128,1024]{1,0:T(8,128)(2,1)}) %reduce-scatter.2.cloned.1.call-update) | async-done | bytes 262160 | tf_op jit(solution)/shard_map/reduce_scatter | solution.py:119
  (1098 shorter events, 391.3 us)
Async XLA Ops:
  6.5 478.9 %all-gather.2.cloned.1.call-start = ((), (), s32[]{:S(2)}) async-start(), calls=%async_computation.1 | async-start | bytes 4456448 | tf_op jit(solution)/shard_map/all_gather | solution.py:115
  24.0 10.9 %collective-permute-start.3 = (bf16[64,1,16,128]{3,0,2,1:T(8,128)(2,1)S(1)}, bf16[64,1,16,128]{3,0,2,1:T(8,128)(2,1)S(1)}, u32[]{:S(2)}, u32[]{:S(2)}) collective-permute-start(bf16[64,1,16,128]{3,0,2,1:T(8,128)(2,1)S(1)} %convert_element_type.124), channel_id=1, source_target_pairs={{120,0},{0,8},{8,16},{16,24},{24,32},{32,40},{40,48},{48,56},{56,6... | collective-permute-start | bytes 786440 | tf_op jit(solution)/shard_map/while/body/eval_jaxpr/ppermute | solution.py:20
  51.4 10.9 %collective-permute-start.3 = (bf16[64,1,16,128]{3,0,2,1:T(8,128)(2,1)S(1)}, bf16[64,1,16,128]{3,0,2,1:T(8,128)(2,1)S(1)}, u32[]{:S(2)}, u32[]{:S(2)}) collective-permute-start(bf16[64,1,16,128]{3,0,2,1:T(8,128)(2,1)S(1)} %convert_element_type.124), channel_id=1, source_target_pairs={{120,0},{0,8},{8,16},{16,24},{24,32},{32,40},{40,48},{48,56},{56,6... | collective-permute-start | bytes 786440 | tf_op jit(solution)/shard_map/while/body/eval_jaxpr/ppermute | solution.py:20
  78.9 10.9 %collective-permute-start.3 = (bf16[64,1,16,128]{3,0,2,1:T(8,128)(2,1)S(1)}, bf16[64,1,16,128]{3,0,2,1:T(8,128)(2,1)S(1)}, u32[]{:S(2)}, u32[]{:S(2)}) collective-permute-start(bf16[64,1,16,128]{3,0,2,1:T(8,128)(2,1)S(1)} %convert_element_type.124), channel_id=1, source_target_pairs={{120,0},{0,8},{8,16},{16,24},{24,32},{32,40},{40,48},{48,56},{56,6... | collective-permute-start | bytes 786440 | tf_op jit(solution)/shard_map/while/body/eval_jaxpr/ppermute | solution.py:20
  79.0 10.8 %collective-permute-start = (bf16[64,2048]{1,0:T(8,128)(2,1)S(1)}, bf16[64,2048]{1,0:T(8,128)(2,1)S(1)}, u32[]{:S(2)}, u32[]{:S(2)}) collective-permute-start(bf16[64,2048]{1,0:T(8,128)(2,1)S(1)} %copy.35), channel_id=1, source_target_pairs={{120,0},{0,8},{8,16},{16,24},{24,32},{32,40},{40,48},{48,56},{56,6... | collective-permute-start | bytes 786440 | tf_op jit(solution)/shard_map/while/body/eval_jaxpr/ppermute | solution.py:20
  106.4 10.9 %collective-permute-start.3 = (bf16[64,1,16,128]{3,0,2,1:T(8,128)(2,1)S(1)}, bf16[64,1,16,128]{3,0,2,1:T(8,128)(2,1)S(1)}, u32[]{:S(2)}, u32[]{:S(2)}) collective-permute-start(bf16[64,1,16,128]{3,0,2,1:T(8,128)(2,1)S(1)} %convert_element_type.124), channel_id=1, source_target_pairs={{120,0},{0,8},{8,16},{16,24},{24,32},{32,40},{40,48},{48,56},{56,6... | collective-permute-start | bytes 786440 | tf_op jit(solution)/shard_map/while/body/eval_jaxpr/ppermute | solution.py:20
  106.4 10.8 %collective-permute-start = (bf16[64,2048]{1,0:T(8,128)(2,1)S(1)}, bf16[64,2048]{1,0:T(8,128)(2,1)S(1)}, u32[]{:S(2)}, u32[]{:S(2)}) collective-permute-start(bf16[64,2048]{1,0:T(8,128)(2,1)S(1)} %copy.35), channel_id=1, source_target_pairs={{120,0},{0,8},{8,16},{16,24},{24,32},{32,40},{40,48},{48,56},{56,6... | collective-permute-start | bytes 786440 | tf_op jit(solution)/shard_map/while/body/eval_jaxpr/ppermute | solution.py:20
  133.8 10.9 %collective-permute-start.3 = (bf16[64,1,16,128]{3,0,2,1:T(8,128)(2,1)S(1)}, bf16[64,1,16,128]{3,0,2,1:T(8,128)(2,1)S(1)}, u32[]{:S(2)}, u32[]{:S(2)}) collective-permute-start(bf16[64,1,16,128]{3,0,2,1:T(8,128)(2,1)S(1)} %convert_element_type.124), channel_id=1, source_target_pairs={{120,0},{0,8},{8,16},{16,24},{24,32},{32,40},{40,48},{48,56},{56,6... | collective-permute-start | bytes 786440 | tf_op jit(solution)/shard_map/while/body/eval_jaxpr/ppermute | solution.py:20
  133.9 10.8 %collective-permute-start = (bf16[64,2048]{1,0:T(8,128)(2,1)S(1)}, bf16[64,2048]{1,0:T(8,128)(2,1)S(1)}, u32[]{:S(2)}, u32[]{:S(2)}) collective-permute-start(bf16[64,2048]{1,0:T(8,128)(2,1)S(1)} %copy.35), channel_id=1, source_target_pairs={{120,0},{0,8},{8,16},{16,24},{24,32},{32,40},{40,48},{48,56},{56,6... | collective-permute-start | bytes 786440 | tf_op jit(solution)/shard_map/while/body/eval_jaxpr/ppermute | solution.py:20
  161.3 10.9 %collective-permute-start.3 = (bf16[64,1,16,128]{3,0,2,1:T(8,128)(2,1)S(1)}, bf16[64,1,16,128]{3,0,2,1:T(8,128)(2,1)S(1)}, u32[]{:S(2)}, u32[]{:S(2)}) collective-permute-start(bf16[64,1,16,128]{3,0,2,1:T(8,128)(2,1)S(1)} %convert_element_type.124), channel_id=1, source_target_pairs={{120,0},{0,8},{8,16},{16,24},{24,32},{32,40},{40,48},{48,56},{56,6... | collective-permute-start | bytes 786440 | tf_op jit(solution)/shard_map/while/body/eval_jaxpr/ppermute | solution.py:20
  161.4 10.8 %collective-permute-start = (bf16[64,2048]{1,0:T(8,128)(2,1)S(1)}, bf16[64,2048]{1,0:T(8,128)(2,1)S(1)}, u32[]{:S(2)}, u32[]{:S(2)}) collective-permute-start(bf16[64,2048]{1,0:T(8,128)(2,1)S(1)} %copy.35), channel_id=1, source_target_pairs={{120,0},{0,8},{8,16},{16,24},{24,32},{32,40},{40,48},{48,56},{56,6... | collective-permute-start | bytes 786440 | tf_op jit(solution)/shard_map/while/body/eval_jaxpr/ppermute | solution.py:20
  188.8 10.9 %collective-permute-start.3 = (bf16[64,1,16,128]{3,0,2,1:T(8,128)(2,1)S(1)}, bf16[64,1,16,128]{3,0,2,1:T(8,128)(2,1)S(1)}, u32[]{:S(2)}, u32[]{:S(2)}) collective-permute-start(bf16[64,1,16,128]{3,0,2,1:T(8,128)(2,1)S(1)} %convert_element_type.124), channel_id=1, source_target_pairs={{120,0},{0,8},{8,16},{16,24},{24,32},{32,40},{40,48},{48,56},{56,6... | collective-permute-start | bytes 786440 | tf_op jit(solution)/shard_map/while/body/eval_jaxpr/ppermute | solution.py:20
  188.9 10.8 %collective-permute-start = (bf16[64,2048]{1,0:T(8,128)(2,1)S(1)}, bf16[64,2048]{1,0:T(8,128)(2,1)S(1)}, u32[]{:S(2)}, u32[]{:S(2)}) collective-permute-start(bf16[64,2048]{1,0:T(8,128)(2,1)S(1)} %copy.35), channel_id=1, source_target_pairs={{120,0},{0,8},{8,16},{16,24},{24,32},{32,40},{40,48},{48,56},{56,6... | collective-permute-start | bytes 786440 | tf_op jit(solution)/shard_map/while/body/eval_jaxpr/ppermute | solution.py:20
  216.2 10.9 %collective-permute-start.3 = (bf16[64,1,16,128]{3,0,2,1:T(8,128)(2,1)S(1)}, bf16[64,1,16,128]{3,0,2,1:T(8,128)(2,1)S(1)}, u32[]{:S(2)}, u32[]{:S(2)}) collective-permute-start(bf16[64,1,16,128]{3,0,2,1:T(8,128)(2,1)S(1)} %convert_element_type.124), channel_id=1, source_target_pairs={{120,0},{0,8},{8,16},{16,24},{24,32},{32,40},{40,48},{48,56},{56,6... | collective-permute-start | bytes 786440 | tf_op jit(solution)/shard_map/while/body/eval_jaxpr/ppermute | solution.py:20
  216.3 10.8 %collective-permute-start = (bf16[64,2048]{1,0:T(8,128)(2,1)S(1)}, bf16[64,2048]{1,0:T(8,128)(2,1)S(1)}, u32[]{:S(2)}, u32[]{:S(2)}) collective-permute-start(bf16[64,2048]{1,0:T(8,128)(2,1)S(1)} %copy.35), channel_id=1, source_target_pairs={{120,0},{0,8},{8,16},{16,24},{24,32},{32,40},{40,48},{48,56},{56,6... | collective-permute-start | bytes 786440 | tf_op jit(solution)/shard_map/while/body/eval_jaxpr/ppermute | solution.py:20
  243.7 10.9 %collective-permute-start.3 = (bf16[64,1,16,128]{3,0,2,1:T(8,128)(2,1)S(1)}, bf16[64,1,16,128]{3,0,2,1:T(8,128)(2,1)S(1)}, u32[]{:S(2)}, u32[]{:S(2)}) collective-permute-start(bf16[64,1,16,128]{3,0,2,1:T(8,128)(2,1)S(1)} %convert_element_type.124), channel_id=1, source_target_pairs={{120,0},{0,8},{8,16},{16,24},{24,32},{32,40},{40,48},{48,56},{56,6... | collective-permute-start | bytes 786440 | tf_op jit(solution)/shard_map/while/body/eval_jaxpr/ppermute | solution.py:20
  271.2 10.9 %collective-permute-start.3 = (bf16[64,1,16,128]{3,0,2,1:T(8,128)(2,1)S(1)}, bf16[64,1,16,128]{3,0,2,1:T(8,128)(2,1)S(1)}, u32[]{:S(2)}, u32[]{:S(2)}) collective-permute-start(bf16[64,1,16,128]{3,0,2,1:T(8,128)(2,1)S(1)} %convert_element_type.124), channel_id=1, source_target_pairs={{120,0},{0,8},{8,16},{16,24},{24,32},{32,40},{40,48},{48,56},{56,6... | collective-permute-start | bytes 786440 | tf_op jit(solution)/shard_map/while/body/eval_jaxpr/ppermute | solution.py:20
  298.6 10.9 %collective-permute-start.3 = (bf16[64,1,16,128]{3,0,2,1:T(8,128)(2,1)S(1)}, bf16[64,1,16,128]{3,0,2,1:T(8,128)(2,1)S(1)}, u32[]{:S(2)}, u32[]{:S(2)}) collective-permute-start(bf16[64,1,16,128]{3,0,2,1:T(8,128)(2,1)S(1)} %convert_element_type.124), channel_id=1, source_target_pairs={{120,0},{0,8},{8,16},{16,24},{24,32},{32,40},{40,48},{48,56},{56,6... | collective-permute-start | bytes 786440 | tf_op jit(solution)/shard_map/while/body/eval_jaxpr/ppermute | solution.py:20
  326.1 10.9 %collective-permute-start.3 = (bf16[64,1,16,128]{3,0,2,1:T(8,128)(2,1)S(1)}, bf16[64,1,16,128]{3,0,2,1:T(8,128)(2,1)S(1)}, u32[]{:S(2)}, u32[]{:S(2)}) collective-permute-start(bf16[64,1,16,128]{3,0,2,1:T(8,128)(2,1)S(1)} %convert_element_type.124), channel_id=1, source_target_pairs={{120,0},{0,8},{8,16},{16,24},{24,32},{32,40},{40,48},{48,56},{56,6... | collective-permute-start | bytes 786440 | tf_op jit(solution)/shard_map/while/body/eval_jaxpr/ppermute | solution.py:20
  353.6 10.9 %collective-permute-start.3 = (bf16[64,1,16,128]{3,0,2,1:T(8,128)(2,1)S(1)}, bf16[64,1,16,128]{3,0,2,1:T(8,128)(2,1)S(1)}, u32[]{:S(2)}, u32[]{:S(2)}) collective-permute-start(bf16[64,1,16,128]{3,0,2,1:T(8,128)(2,1)S(1)} %convert_element_type.124), channel_id=1, source_target_pairs={{120,0},{0,8},{8,16},{16,24},{24,32},{32,40},{40,48},{48,56},{56,6... | collective-permute-start | bytes 786440 | tf_op jit(solution)/shard_map/while/body/eval_jaxpr/ppermute | solution.py:20
  381.1 10.9 %collective-permute-start.3 = (bf16[64,1,16,128]{3,0,2,1:T(8,128)(2,1)S(1)}, bf16[64,1,16,128]{3,0,2,1:T(8,128)(2,1)S(1)}, u32[]{:S(2)}, u32[]{:S(2)}) collective-permute-start(bf16[64,1,16,128]{3,0,2,1:T(8,128)(2,1)S(1)} %convert_element_type.124), channel_id=1, source_target_pairs={{120,0},{0,8},{8,16},{16,24},{24,32},{32,40},{40,48},{48,56},{56,6... | collective-permute-start | bytes 786440 | tf_op jit(solution)/shard_map/while/body/eval_jaxpr/ppermute | solution.py:20
  408.5 10.9 %collective-permute-start.3 = (bf16[64,1,16,128]{3,0,2,1:T(8,128)(2,1)S(1)}, bf16[64,1,16,128]{3,0,2,1:T(8,128)(2,1)S(1)}, u32[]{:S(2)}, u32[]{:S(2)}) collective-permute-start(bf16[64,1,16,128]{3,0,2,1:T(8,128)(2,1)S(1)} %convert_element_type.124), channel_id=1, source_target_pairs={{120,0},{0,8},{8,16},{16,24},{24,32},{32,40},{40,48},{48,56},{56,6... | collective-permute-start | bytes 786440 | tf_op jit(solution)/shard_map/while/body/eval_jaxpr/ppermute | solution.py:20
  436.0 10.9 %collective-permute-start.3 = (bf16[64,1,16,128]{3,0,2,1:T(8,128)(2,1)S(1)}, bf16[64,1,16,128]{3,0,2,1:T(8,128)(2,1)S(1)}, u32[]{:S(2)}, u32[]{:S(2)}) collective-permute-start(bf16[64,1,16,128]{3,0,2,1:T(8,128)(2,1)S(1)} %convert_element_type.124), channel_id=1, source_target_pairs={{120,0},{0,8},{8,16},{16,24},{24,32},{32,40},{40,48},{48,56},{56,6... | collective-permute-start | bytes 786440 | tf_op jit(solution)/shard_map/while/body/eval_jaxpr/ppermute | solution.py:20
  448.1 123.5 %reduce-scatter.2.cloned.1.call-start = ((), (), s32[]{:S(2)}) async-start(), calls=%async_computation.2 | async-start | bytes 2359296 | tf_op jit(solution)/shard_map/reduce_scatter | solution.py:119
  (59 other events, 549.5 us)
Sparse Core Ops, SparseCore 0:
  448.3 37.1 all-gather.1
  494.8 76.7 reduce-scatter.1
where the time goes:
time: 582 us; the launch traced here: 580 us
  waiting for transfers between devices  277 us (48%)
  other arithmetic  97.3 us (17%)
  matrix products  89.2 us (15%)
  local copies, waits for them, and re-layouts  83.9 us (14%)
  between operations  13.4 us (2%)
  starting transfers between devices  10.3 us (2%)
  loops' own time  8.94 us (2%)
    ppermute x64, waiting for transfers between devices, shifted(): return lax.ppermute(block, axis, route)  163 us
    reduce_scatter x1, waiting for transfers between devices, shards(): lax.psum_scatter(partial_rows.astype(jnp.bfloat16), 'heads', scatter_dime...  76.9 us
    dot_general x64, matrix products, one_block(): jnp.einsum('rkgj,jkd->rkgd', weights.astype(jnp.bfloat16), value_block, p...  46.1 us
    reduce_sum x64, other arithmetic, one_block(): weight_sum = weight_sum * keeping + jnp.sum(weights, axis=3)  44.4 us
    lt x64, other arithmetic, one_block(): key_pos[None, :] < limits[1]  40.9 us
    slice x64, local copies, waits for them, and re-layouts, one_block(): limits[1]  38.7 us
    all_gather x1, waiting for transfers between devices, shards(): lax.all_gather(attended, 'ctx', axis=0, tiled=True)  37.2 us
    dot_general x64, matrix products, one_block(): jnp.einsum('rkgd,jkd->rkgj', shaped_query, key_block, preferred_element_t...  33.9 us
  transfers between devices with their start and end apart: 66, of which 18 were waited for; matrix products, arithmetic and copies ran while one was open for 0% of the time, Pallas kernels for 0%

commit v1 on v0

v1 whole, which is shorter than its diff:
```python
import functools
import math

import jax
import jax.numpy as jnp
from jax import lax
from jax.experimental import pallas as pl
from jax.experimental.pallas import tpu as pltpu
from jax.sharding import PartitionSpec as P

H = 128
KV = 8
HD = 128
Q = 512
GROUPS = H // KV
NEG = -1e30
LOG2E = 1.4426950408889634
SCALE2 = LOG2E / math.sqrt(HD)
CHIPS = 8
HALF = GROUPS // 2
BF16 = jnp.bfloat16
F32 = jnp.float32
MESH = pl.DeviceIdType.MESH


def chip_offset(k):
    return k // 2, (k + (k + 6) // 8) % 2


def kernel(
    bounds, q_ref, k_hbm, v_hbm, w_hbm, res_ref, out_ref,
    q_all, k_buf, v_buf, w_buf, s_a, s_b, m_a, m_b,
    o_all, lse_all, rc, rc_lse, mx, mx_lse, rx, rx_lse,
    att, pp, ry, zs, rz,
    local_sem, q_send, q_recv, qf_send,
    c_send, c_recv, cl_send, cl_recv,
    x_send, x_recv, xl_send, xl_recv,
    a_send, a_recv, af_send, y_send, y_recv, z_send, z_recv,
):
    me = lax.axis_index("ctx")
    hd = lax.axis_index("heads")
    x, zl, c = me // 4, (me // 2) % 2, me % 2
    zh, y = hd // 4, hd % 4
    rows = q_ref.shape[0]
    span = k_buf.shape[1]
    half_rows = HALF * rows

    def ctx_at(dx, dz, dc):
        return ((x + dx) % 4) * 4 + ((zl + dz) % 2) * 2 + (c + dc) % 2

    partner = ctx_at(0, 0, 1)

    def remote(src, dst, send, recv, **where):
        return pltpu.make_async_remote_copy(
            src_ref=src, dst_ref=dst, send_sem=send, recv_sem=recv,
            device_id=where, device_id_type=MESH,
        )

    load_k = pltpu.make_async_copy(k_hbm, k_buf, local_sem.at[0])
    load_v = pltpu.make_async_copy(v_hbm, v_buf.at[:, :, pl.ds(0, HD)], local_sem.at[1])
    load_w = pltpu.make_async_copy(w_hbm, w_buf, local_sem.at[2])
    load_k.start()
    load_v.start()
    load_w.start()

    barrier = pltpu.get_barrier_semaphore()
    pl.semaphore_signal(barrier, inc=1, device_id={"ctx": partner}, device_id_type=MESH)
    for k in range(1, CHIPS):
        dx, dz = chip_offset(k)
        pl.semaphore_signal(barrier, inc=1, device_id={"ctx": ctx_at(dx, dz, 0)}, device_id_type=MESH)
    for dy in range(1, 4):
        pl.semaphore_signal(barrier, inc=1, device_id={"heads": zh * 4 + (y + dy) % 4}, device_id_type=MESH)
    pl.semaphore_signal(barrier, inc=1, device_id={"heads": (1 - zh) * 4 + y}, device_id_type=MESH)
    q_all[0] = q_ref[...]
    for p in range(2):
        v_buf[p, :, pl.ds(HD, HD)] = jnp.ones((span, HD), BF16)
    pl.semaphore_wait(barrier, 1 + (CHIPS - 1) + 3 + 1)

    def q_own(k):
        dx, dz = chip_offset(k)
        return remote(q_ref, q_all.at[2 * k], q_send.at[k], q_recv.at[2 * k], ctx=ctx_at(-dx, -dz, 0))

    q_pair = remote(q_ref, q_all.at[1], q_send.at[0], q_recv.at[1], ctx=partner)
    q_pair.start()
    for k in range(1, CHIPS):
        q_own(k).start()

    def q_forward(k):
        return remote(q_all.at[2 * k], q_all.at[2 * k + 1], qf_send.at[k], q_recv.at[2 * k + 1], ctx=partner)

    load_k.wait()

    def place(n):
        k = n // 2
        dx, dz = chip_offset(k)
        t = ctx_at(dx, dz, n % 2)
        return t // 8, (t % 8) * rows

    def scores(n, half, s_ref, m_ref):
        p, within = place(n)
        block = jnp.concatenate(
            [q_all[n, :, pl.ds((half * HALF + j) * HD, HD)] for j in range(HALF)], axis=0
        )
        s = lax.dot_general(
            block, k_buf[p], (((1,), (1,)), ((), ())), preferred_element_type=F32
        )
        row = lax.broadcasted_iota(jnp.int32, (rows, 1), 0)
        limit = jnp.minimum(bounds[p, 0] + within + row, bounds[p, 1] - 1) - me * span
        limit = jnp.concatenate([limit] * HALF, axis=0)
        key = lax.broadcasted_iota(jnp.int32, (half_rows, span), 1)
        s = jnp.where(key <= limit, s, NEG)
        s_ref[...] = s
        m_ref[...] = jnp.broadcast_to(jnp.max(s, axis=1, keepdims=True), (half_rows, HD))

    def mix(n, half, s_ref, m_ref):
        p, _ = place(n)
        m = m_ref[...]
        weights = jnp.exp2((s_ref[...] - jnp.concatenate([m] * (span // HD), axis=1)) * SCALE2)
        both = jnp.dot(weights.astype(BF16), v_buf[p], preferred_element_type=F32)
        total = both[:, HD:]
        mixed = (both[:, :HD] / total).astype(BF16)
        lane = lax.broadcasted_iota(jnp.int32, (rows, HD), 1)
        m_c = jnp.zeros((rows, HD), F32)
        t_c = jnp.ones((rows, HD), F32)
        for j in range(HALF):
            h = half * HALF + j
            part = slice(j * rows, (j + 1) * rows)
            o_all[n, :, pl.ds(h * HD, HD)] = mixed[part]
            m_c = jnp.where(lane == h, m[part], m_c)
            t_c = jnp.where(lane == h, total[part], t_c)
        lse = m_c * SCALE2 + jnp.log(t_c) * LOG2E
        if half:
            lse = jnp.where(lane >= HALF, lse, lse_all[n])
        lse_all[n] = lse

    def merge(parts, out, out_lse):
        lses = [lse[...] for _, lse in parts]
        top = functools.reduce(jnp.maximum, lses)
        es = [jnp.exp2(lse - top) for lse in lses]
        tot = functools.reduce(lambda a, b: a + b, es)
        inv = 1.0 / tot
        if out_lse is not None:
            out_lse[...] = top + jnp.log(tot) * LOG2E
        ws = [e * inv for e in es]
        for h in range(GROUPS):
            cols = pl.ds(h * HD, HD)
            acc = None
            for (o, _), w in zip(parts, ws):
                term = o[:, cols].astype(F32) * jnp.broadcast_to(w[:, h:h + 1], (rows, HD))
                acc = term if acc is None else acc + term
            out[:, cols] = acc.astype(BF16)

    def pair_send(k):
        return (
            remote(o_all.at[2 * k + 1], rc.at[k], c_send.at[k], c_recv.at[k], ctx=partner),
            remote(lse_all.at[2 * k + 1], rc_lse.at[k], cl_send.at[k], cl_recv.at[k], ctx=partner),
        )

    def owner_send(k):
        dx, dz = chip_offset(k)
        to = ctx_at(dx, dz, 0)
        return (
            remote(mx.at[k], rx.at[k], x_send.at[k], x_recv.at[k], ctx=to),
            remote(mx_lse.at[k], rx_lse.at[k], xl_send.at[k], xl_recv.at[k], ctx=to),
        )

    def merge_pair(k):
        for copy in pair_send(k):
            copy.wait_recv()
        merge(
            [(o_all.at[2 * k], lse_all.at[2 * k]), (rc.at[k], rc_lse.at[k])],
            mx.at[k], mx_lse.at[k],
        )

    scores(0, 0, s_a, m_a)
    load_v.wait()
    steps = 2 * CHIPS

    def step(n, _):
        mix(n, 0, s_a, m_a)
        scores(n, 1, s_b, m_b)
        nxt = jnp.minimum(n + 1, steps - 1)

        @pl.when(n < steps - 1)
        def _():
            q_own_like(nxt).wait_recv()

        @pl.when((n % 2 == 1) & (n < steps - 1))
        def _():
            q_forward((n + 1) // 2).start()

        scores(nxt, 0, s_a, m_a)
        mix(n, 1, s_b, m_b)

        @pl.when(n % 2 == 1)
        def _():
            for copy in pair_send(n // 2):
                copy.start()

        @pl.when((n % 2 == 0) & (n >= 2))
        def _():
            k = n // 2 - 1
            merge_pair(k)

            @pl.when(k > 0)
            def _():
                for copy in owner_send(k):
                    copy.start()

        return 0

    def q_own_like(n):
        return remote(q_all.at[n], q_all.at[n], qf_send.at[0], q_recv.at[n], ctx=partner)

    lax.fori_loop(0, steps, step, 0)

    last = CHIPS - 1
    merge_pair(last)
    for copy in owner_send(last):
        copy.start()
    for k in range(1, CHIPS):
        for copy in owner_send(k):
            copy.wait_recv()
    merge(
        [(mx.at[0], mx_lse.at[0])] + [(rx.at[k], rx_lse.at[k]) for k in range(1, CHIPS)],
        att.at[0], None,
    )

    def a_own(k):
        dx, dz = chip_offset(k)
        return remote(att.at[0], att.at[2 * k], a_send.at[k], a_recv.at[2 * k], ctx=ctx_at(-dx, -dz, 0))

    def a_wait(n):
        return remote(att.at[n], att.at[n], af_send.at[0], a_recv.at[n], ctx=partner)

    def a_forward(k):
        return remote(att.at[2 * k], att.at[2 * k + 1], af_send.at[k], a_recv.at[2 * k + 1], ctx=partner)

    a_pair = remote(att.at[0], att.at[1], a_send.at[0], a_recv.at[1], ctx=partner)
    a_pair.start()
    for k in range(1, CHIPS):
        a_own(k).start()
    load_w.wait()

    def y_copy(k):
        dx, dz = chip_offset(k)
        hp = ((x + dx) % 4) * 2 + (zl + dz) % 2
        zp, yp = hp // 4, hp % 4
        return yp, zp, remote(pp.at[k], ry.at[zp, y], y_send.at[k], y_recv.at[zp, y], heads=zh * 4 + yp)

    def project(k, _):
        @pl.when(k < last)
        def _():
            a_wait(2 * k + 2).wait_recv()
            a_forward(k + 1).start()

        a_wait(2 * k + 1).wait_recv()
        both = jnp.concatenate([att[2 * k], att[2 * k + 1]], axis=0)
        done = jnp.dot(both, w_buf[...], preferred_element_type=F32).astype(BF16)
        pp[k, pl.ds(pl.multiple_of(c * rows, rows), rows), :] = done[:rows]
        pp[k, pl.ds(pl.multiple_of((1 - c) * rows, rows), rows), :] = done[rows:]
        yp, zp, copy = y_copy(k)

        @pl.when(yp != y)
        def _():
            copy.start()

        @pl.when(yp == y)
        def _():
            ry[zp, y] = pp[k]

        return 0

    lax.fori_loop(0, CHIPS, project, 0)

    def y_wait(zp, dy):
        ys = (y + dy) % 4
        return remote(ry.at[zp, ys], ry.at[zp, ys], y_send.at[0], y_recv.at[zp, ys], heads=zh * 4 + ys)

    far = 1 - zh
    for dy in range(1, 4):
        y_wait(far, dy).wait_recv()
    total = ry[far, 0].astype(F32)
    for ys in range(1, 4):
        total = total + ry[far, ys].astype(F32)
    zs[...] = total.astype(BF16)
    z_copy = remote(zs, rz, z_send, z_recv, heads=far * 4 + y)
    z_copy.start()
    for dy in range(1, 4):
        y_wait(zh, dy).wait_recv()
    total = res_ref[...].astype(F32)
    for ys in range(4):
        total = total + ry[zh, ys].astype(F32)
    z_copy.wait_recv()
    out_ref[...] = (total + rz[...].astype(F32)).astype(BF16)

    q_pair.wait_send()
    a_pair.wait_send()
    z_copy.wait_send()

    def drain(k, _):
        q_own(k).wait_send()
        q_forward(k).wait_send()
        a_own(k).wait_send()
        a_forward(k).wait_send()
        for copy in owner_send(k):
            copy.wait_send()
        return 0

    lax.fori_loop(1, CHIPS, drain, 0)

    def drain_all(k, _):
        for copy in pair_send(k):
            copy.wait_send()
        yp, _, copy = y_copy(k)

        @pl.when(yp != y)
        def _():
            copy.wait_send()

        return 0

    lax.fori_loop(0, CHIPS, drain_all, 0)


def shards(queries, cache_keys, cache_values, bounds, out_weight, residual):
    rows, cols = queries.shape
    prompts, span, hd = cache_keys.shape
    out_rows, width = residual.shape
    vmem = pl.BlockSpec(memory_space=pltpu.VMEM)
    hbm = pl.BlockSpec(memory_space=pl.ANY)
    n = 2 * CHIPS
    half_rows = HALF * rows
    dma = lambda *s: pltpu.SemaphoreType.DMA(s)
    return pl.pallas_call(
        kernel,
        out_shape=jax.ShapeDtypeStruct(residual.shape, BF16),
        in_specs=[pl.BlockSpec(memory_space=pltpu.SMEM), vmem, hbm, hbm, hbm, vmem],
        out_specs=vmem,
        scratch_shapes=[
            pltpu.VMEM((n, rows, cols), BF16),
            pltpu.VMEM((prompts, span, hd), BF16),
            pltpu.VMEM((prompts, span, 2 * hd), BF16),
            pltpu.VMEM(out_weight.shape, BF16),
            pltpu.VMEM((half_rows, span), F32),
            pltpu.VMEM((half_rows, span), F32),
            pltpu.VMEM((half_rows, hd), F32),
            pltpu.VMEM((half_rows, hd), F32),
            pltpu.VMEM((n, rows, cols), BF16),
            pltpu.VMEM((n, rows, hd), F32),
            pltpu.VMEM((CHIPS, rows, cols), BF16),
            pltpu.VMEM((CHIPS, rows, hd), F32),
            pltpu.VMEM((CHIPS, rows, cols), BF16),
            pltpu.VMEM((CHIPS, rows, hd), F32),
            pltpu.VMEM((CHIPS, rows, cols), BF16),
            pltpu.VMEM((CHIPS, rows, hd), F32),
            pltpu.VMEM((n, rows, cols), BF16),
            pltpu.VMEM((CHIPS, out_rows, width), BF16),
            pltpu.VMEM((2, 4, out_rows, width), BF16),
            pltpu.VMEM((out_rows, width), BF16),
            pltpu.VMEM((out_rows, width), BF16),
            dma(3), dma(CHIPS), dma(n), dma(CHIPS),
            dma(CHIPS), dma(CHIPS), dma(CHIPS), dma(CHIPS),
            dma(CHIPS), dma(CHIPS), dma(CHIPS), dma(CHIPS),
            dma(CHIPS), dma(n), dma(CHIPS), dma(CHIPS), dma(2, 4),
            pltpu.SemaphoreType.DMA, pltpu.SemaphoreType.DMA,
        ],
        compiler_params=pltpu.CompilerParams(
            collective_id=0, has_side_effects=True, vmem_limit_bytes=62 * 1024 * 1024
        ),
    )(bounds, queries, cache_keys, cache_values, out_weight, residual)


def solution(mesh):
    in_specs = (
        P("ctx", "heads"),
        P(None, "ctx", "heads"),
        P(None, "ctx", "heads"),
        P(),
        P("heads", "ctx"),
        P("heads", "ctx"),
    )
    out_specs = P("heads", "ctx")
    return jax.shard_map(shards, mesh=mesh, in_specs=in_specs, out_specs=out_specs, check_vma=False)
```

time: 582 us -> 161 us (0.28)
  the two profiles are of different devices: /device:TPU:0 before, /device:TPU:30 now
where the time goes in v1:
time: 161 us
  Pallas kernels  159 us (99%)
  local copies, waits for them, and re-layouts  1.67 us (1%)
    pallas_call x1, Pallas kernels, shards(): pl.pallas_call(kernel, out_shape=jax.ShapeDtypeStruct(residual.shape, BF1...  159 us

profile of v1, /device:TPU:30, one launch (start us, length us, event | category | flops | bytes accessed | tf_op | source)
XLA Modules:
  0.0 160.8 jit_solution(1066548700700202366)
XLA Ops:
  0.0 159.1 %shard_map.64 = bf16[128,1024]{1,0:T(8,128)(2,1)} custom-call(s32[2,2]{1,0:T(2,128)} %bounds.1, bf16[64,2048]{1,0:T(8,128)(2,1)} %q_ref.1, bf16[2,2048,128]{2,1,0:T(8,128)(2,1)} %k_hbm.1, bf16[2,2048,128]{2,1,0:T(8,128)(2,1)} %v_hbm.1, bf16[2048,1024]{1,0:T(8,128)(2,1)} %w_hbm.1, bf16[128,1024]{1,0:T(8,128)(2,1)} %res_ref.1), custom_call_target="tpu_custom_call" | custom-call | tf_op jit(solution)/shard_map/pallas_call | solution.py:335
  159.1 1.7 %copy.8 = bf16[128,1024]{1,0:T(8,128)(2,1)} copy(bf16[128,1024]{1,0:T(8,128)(2,1)} %shard_map.64) | data formatting | bytes 524288

commit v2 on v0

v2 whole, which is shorter than its diff:
```python
import functools
import math

import jax
import jax.numpy as jnp
from jax import lax
from jax.experimental import pallas as pl
from jax.experimental.pallas import tpu as pltpu
from jax.sharding import PartitionSpec as P

H = 128
KV = 8
HD = 128
GROUPS = H // KV
NEG = -1e30
LOG2E = 1.4426950408889634
SCALE2 = LOG2E / math.sqrt(HD)
CHIPS = 8
SUBS = 2
LAST = SUBS * CHIPS - 1
BF16 = jnp.bfloat16
F32 = jnp.float32
MESH = pl.DeviceIdType.MESH
OFFSETS = ((0, 0), (0, 1), (1, 0), (3, 0), (2, 0), (2, 1), (1, 1), (3, 1))


def pick(k, values):
    if isinstance(k, int):
        return values[k]
    out = values[0]
    for j in range(1, len(values)):
        out = jnp.where(k == j, values[j], out)
    return out


def offset(k):
    return pick(k, [o[0] for o in OFFSETS]), pick(k, [o[1] for o in OFFSETS])


def sub_and_pair(m):
    rest = m - SUBS
    if isinstance(m, int):
        return (m, 0) if m < SUBS else (rest // (CHIPS - 1), rest % (CHIPS - 1) + 1)
    own = m < SUBS
    rest = jnp.maximum(rest, 0)
    return (
        jnp.where(own, m, rest // (CHIPS - 1)),
        jnp.where(own, 0, rest % (CHIPS - 1) + 1),
    )


def step_of(u, k):
    return u if k == 0 else SUBS + (CHIPS - 1) * u + k - 1


def kernel(
    bounds, q_ref, k_hbm, v_hbm, w_hbm, res_ref, out_ref,
    q_all, k_buf, v_buf, w_buf, s_a, s_b, m_a, m_b,
    o_all, lse_all, rc, rc_lse, mx, mx_lse, rx, rx_lse,
    att, pp, yl, yr, ra, rb, zs, rz,
    local_sem, *sems,
):
    q_sems, a_sems, (c_send, c_recv, cl_send, cl_recv), (x_send, x_recv, xl_send, xl_recv), (
        y1_send, y1_recv, y2_send, y2_recv, z_send, z_recv,
    ) = sems[:6], sems[6:12], sems[12:16], sems[16:20], sems[20:]
    me = lax.axis_index("ctx")
    hd = lax.axis_index("heads")
    x, zl, c = me // 4, (me // 2) % 2, me % 2
    zh, y = hd // 4, hd % 4
    hr = q_ref.shape[0] // SUBS
    hh = hr // 2
    span = k_buf.shape[1]
    unit = GROUPS * hr

    def ctx_at(dx, dz, dc):
        return ((x + dx) % 4) * 4 + ((zl + dz) % 2) * 2 + (c + dc) % 2

    partner = ctx_at(0, 0, 1)
    zpart = ctx_at(0, 1, 0)
    right = ctx_at(1, 0, 0)
    left = ctx_at(3, 0, 0)
    up = zh * 4 + (y + 1) % 4
    down = zh * 4 + (y + 3) % 4
    across = (1 - zh) * 4 + y

    def remote(src, dst, send, recv, **where):
        return pltpu.make_async_remote_copy(
            src_ref=src, dst_ref=dst, send_sem=send, recv_sem=recv,
            device_id=where, device_id_type=MESH,
        )

    load_k = pltpu.make_async_copy(k_hbm, k_buf, local_sem.at[0])
    load_v = pltpu.make_async_copy(v_hbm, v_buf.at[:, :, pl.ds(0, HD)], local_sem.at[1])
    load_w = pltpu.make_async_copy(w_hbm, w_buf, local_sem.at[2])
    load_k.start()
    load_v.start()
    load_w.start()

    barrier = pltpu.get_barrier_semaphore()
    pl.semaphore_signal(barrier, inc=1, device_id={"ctx": partner}, device_id_type=MESH)
    for k in range(1, CHIPS):
        dx, dz = offset(k)
        pl.semaphore_signal(barrier, inc=1, device_id={"ctx": ctx_at(dx, dz, 0)}, device_id_type=MESH)
    for to in (up, down, across):
        pl.semaphore_signal(barrier, inc=1, device_id={"heads": to}, device_id_type=MESH)
    for u in range(SUBS):
        q_all[u, 0, 0] = q_ref[pl.ds(u * hr, hr), :]
    for p in range(2):
        v_buf[p, :, pl.ds(HD, HD)] = jnp.ones((span, HD), BF16)
    pl.semaphore_wait(barrier, 1 + (CHIPS - 1) + 3)

    def gather(buf, sems, own):
        s0, sc, sz, sh, rv, rh = sems

        def whole(u, k, dc, send, to, src=None):
            return remote(buf.at[u, k, dc] if src is None else src, buf.at[u, k, dc], send, rv.at[u, k, dc], ctx=to)

        def part(u, k, top, src_k, send, to):
            i = 0 if top else 1
            rows = pl.ds(i * hh, hh)
            return remote(buf.at[u, src_k, 0, rows], buf.at[u, k, 0, rows], send, rh.at[u, k - 4, i], ctx=to)

        def stage(u, k):
            if k == 0:
                src = own(u)
                return [
                    whole(u, 0, 1, s0.at[u, 0], partner, src),
                    whole(u, 1, 0, s0.at[u, 1], zpart, src),
                    whole(u, 3, 0, s0.at[u, 2], right, src),
                    whole(u, 2, 0, s0.at[u, 3], left, src),
                ]
            here = buf.at[u, k, 0]
            out = []
            if k == 2:
                out.append(part(u, 4, False, 2, sh.at[u, 0], left))
                out.append(whole(u, 6, 0, sz.at[u, 0], zpart, here))
            if k == 3:
                out.append(part(u, 4, True, 3, sh.at[u, 1], right))
                out.append(whole(u, 7, 0, sz.at[u, 1], zpart, here))
            if k == 6:
                out.append(part(u, 5, False, 6, sh.at[u, 2], left))
            if k == 7:
                out.append(part(u, 5, True, 7, sh.at[u, 3], right))
            out.append(whole(u, k, 1, sc.at[u, k], partner, here))
            return out

        def arrive(u, k):
            if k in (4, 5):
                part(u, k, True, k, sh.at[u, 0], right).wait_recv()
                part(u, k, False, k, sh.at[u, 0], left).wait_recv()
            else:
                whole(u, k, 0, s0.at[u, 0], partner).wait_recv()

        def handle(u, k):
            if k:
                arrive(u, k)
            for copy in stage(u, k):
                copy.start()

        def wait_pair(u, k):
            whole(u, k, 1, s0.at[0, 0], partner).wait_recv()

        def drain(u):
            for k in range(CHIPS):
                for copy in stage(u, k):
                    copy.wait_send()

        return handle, wait_pair, drain, stage

    q_handle, q_wait_pair, q_drain, q_stage = gather(q_all, q_sems, lambda u: q_ref.at[pl.ds(u * hr, hr)])
    a_handle, a_wait_pair, a_drain, _ = gather(att, a_sems, lambda u: att.at[u, 0, 0])

    q_handle(0, 0)
    for u in range(1, SUBS):
        q_stage(u, 0)[0].start()

    def q_rest(u):
        for copy in q_stage(u, 0)[1:]:
            copy.start()

    load_k.wait()

    def place(m, dc):
        u, k = sub_and_pair(m)
        dx, dz = offset(k)
        t = ctx_at(dx, dz, dc)
        return t // 8, (t % 8) * (hr * SUBS) + u * hr

    def scores(m, dc, s_ref, m_ref):
        u, k = sub_and_pair(m)
        p, within = place(m, dc)
        block = jnp.concatenate(
            [q_all[u, k, dc, :, pl.ds(j * HD, HD)] for j in range(GROUPS)], axis=0
        )
        s = lax.dot_general(
            block, k_buf[p], (((1,), (1,)), ((), ())), preferred_element_type=F32
        )
        row = lax.broadcasted_iota(jnp.int32, (hr, 1), 0)
        limit = jnp.minimum(bounds[p, 0] + within + row, bounds[p, 1] - 1) - me * span
        limit = jnp.concatenate([limit] * GROUPS, axis=0)
        key = lax.broadcasted_iota(jnp.int32, (unit, span), 1)
        s = jnp.where(key <= limit, s, NEG)
        s_ref[...] = s
        m_ref[...] = jnp.broadcast_to(jnp.max(s, axis=1, keepdims=True), (unit, HD))

    def mix(m, dc, s_ref, m_ref):
        p, _ = place(m, dc)
        top = m_ref[...]
        weights = jnp.exp2((s_ref[...] - jnp.concatenate([top] * (span // HD), axis=1)) * SCALE2)
        both = jnp.dot(weights.astype(BF16), v_buf[p], preferred_element_type=F32)
        total = both[:, HD:]
        mixed = (both[:, :HD] / total).astype(BF16)
        lane = lax.broadcasted_iota(jnp.int32, (hr, HD), 1)
        m_c = jnp.zeros((hr, HD), F32)
        t_c = jnp.ones((hr, HD), F32)
        for h in range(GROUPS):
            part = slice(h * hr, (h + 1) * hr)
            o_all[m, dc, :, pl.ds(h * HD, HD)] = mixed[part]
            m_c = jnp.where(lane == h, top[part], m_c)
            t_c = jnp.where(lane == h, total[part], t_c)
        lse_all[m, dc] = m_c * SCALE2 + jnp.log(t_c) * LOG2E

    def merge(parts, out, out_lse):
        lses = [lse[...] for _, lse in parts]
        top = functools.reduce(jnp.maximum, lses)
        es = [jnp.exp2(lse - top) for lse in lses]
        tot = functools.reduce(lambda a, b: a + b, es)
        inv = 1.0 / tot
        if out_lse is not None:
            out_lse[...] = top + jnp.log(tot) * LOG2E
        ws = [e * inv for e in es]
        for h in range(GROUPS):
            cols = pl.ds(h * HD, HD)
            acc = None
            for (o, _), w in zip(parts, ws):
                term = o[:, cols].astype(F32) * jnp.broadcast_to(w[:, h:h + 1], (hr, HD))
                acc = term if acc is None else acc + term
            out[:, cols] = acc.astype(BF16)

    def pair_send(m):
        return (
            remote(o_all.at[m, 1], rc.at[m], c_send.at[m], c_recv.at[m], ctx=partner),
            remote(lse_all.at[m, 1], rc_lse.at[m], cl_send.at[m], cl_recv.at[m], ctx=partner),
        )

    def owner_send(m):
        _, k = sub_and_pair(m)
        dx, dz = offset(k)
        to = ctx_at(dx, dz, 0)
        return (
            remote(mx.at[m], rx.at[m], x_send.at[m], x_recv.at[m], ctx=to),
            remote(mx_lse.at[m], rx_lse.at[m], xl_send.at[m], xl_recv.at[m], ctx=to),
        )

    def start_pair(m):
        for copy in pair_send(m):
            copy.start()

    def merge_pair(m):
        for copy in pair_send(m):
            copy.wait_recv()
        merge(
            [(o_all.at[m, 0], lse_all.at[m, 0]), (rc.at[m], rc_lse.at[m])],
            mx.at[m], mx_lse.at[m],
        )

    def start_owner(m):
        for copy in owner_send(m):
            copy.start()

    def finish(u):
        for k in range(1, CHIPS):
            for copy in owner_send(step_of(u, k)):
                copy.wait_recv()
        merge(
            [(mx.at[step_of(u, 0)], mx_lse.at[step_of(u, 0)])]
            + [(rx.at[step_of(u, k)], rx_lse.at[step_of(u, k)]) for k in range(1, CHIPS)],
            att.at[u, 0, 0], None,
        )
        a_handle(u, 0)

    def project(u, ks):
        block = jnp.concatenate([att[u, k, dc] for k in ks for dc in range(2)], axis=0)
        done = jnp.dot(block, w_buf[...], preferred_element_type=F32).astype(BF16)
        i = 0
        for k in ks:
            dx, dz = offset(k)
            hp = ((x + dx) % 4) * 2 + (zl + dz) % 2
            for dc in range(2):
                pp[u, hp // 4, hp % 4, (c + dc) % 2] = done[i * hr:(i + 1) * hr]
                i += 1

    def y1_copies(u, zp):
        yy = (y + 2) % 4
        return (
            remote(pp.at[u, zp, yy, 0], yl.at[u, zp], y1_send.at[u, zp, 0], y1_recv.at[u, zp, 0], heads=up),
            remote(pp.at[u, zp, yy, 1], yr.at[u, zp], y1_send.at[u, zp, 1], y1_recv.at[u, zp, 1], heads=down),
        )

    def y2_copies(u, zp):
        return (
            remote(pp.at[u, zp, (y + 1) % 4], ra.at[u, zp], y2_send.at[u, zp, 0], y2_recv.at[u, zp, 0], heads=up),
            remote(pp.at[u, zp, (y + 3) % 4], rb.at[u, zp], y2_send.at[u, zp, 1], y2_recv.at[u, zp, 1], heads=down),
        )

    far = 1 - zh

    def y_first(u):
        for zp in (far, zh):
            for copy in y1_copies(u, zp):
                copy.start()

    def y_second(u):
        for zp in (far, zh):
            for i, (first, second) in enumerate(zip(y1_copies(u, zp), y2_copies(u, zp))):
                first.wait_recv()
                yy = (y + 1 + 2 * i) % 4
                got = (yl, yr)[i]
                pp[u, zp, yy, i] = (pp[u, zp, yy, i].astype(F32) + got[u, zp].astype(F32)).astype(BF16)
                second.start()

    def z_copy(u):
        return remote(zs.at[u], rz.at[u], z_send.at[u], z_recv.at[u], heads=across)

    def y_total(u, zp):
        for copy in y2_copies(u, zp):
            copy.wait_recv()
        return pp[u, zp, y].astype(F32) + ra[u, zp].astype(F32) + rb[u, zp].astype(F32)

    def z_start(u):
        zs[u] = y_total(u, far).astype(BF16)
        z_copy(u).start()

    def emit(u):
        total = y_total(u, zh)
        z_copy(u).wait_recv()
        total = total + rz[u].astype(F32)
        for cc in range(2):
            rows = pl.ds(cc * hr * SUBS + u * hr, hr)
            out_ref[rows, :] = (res_ref[rows, :].astype(F32) + total[cc]).astype(BF16)

    scores(0, 0, s_a, m_a)
    load_v.wait()

    events = {
        1: [lambda: q_handle(0, 1), lambda: q_handle(0, 2), lambda: q_handle(0, 3)],
        3: [lambda: q_handle(0, 4), lambda: q_rest(1)],
        4: [lambda: q_handle(0, 6), lambda: q_handle(0, 7)],
        5: [lambda: q_handle(0, 5)],
        6: [lambda: q_handle(1, 1), lambda: q_handle(1, 2), lambda: q_handle(1, 3)],
        8: [lambda: q_handle(1, 4)],
        9: [lambda: q_handle(1, 6), lambda: q_handle(1, 7)],
        11: [lambda: q_handle(1, 5)],
        12: [lambda: finish(0)],
        14: [lambda: a_handle(0, 1), lambda: a_handle(0, 2), lambda: a_handle(0, 3)],
        15: [lambda: a_handle(0, 4)],
    }

    def step(m, _):
        for at, acts in events.items():
            @pl.when(m == at)
            def _():
                for act in acts:
                    act()

        u, k = sub_and_pair(m)
        q_wait_pair(u, k)

        @pl.when(m >= 1)
        def _():
            start_pair(m - 1)

        @pl.when(m >= 2)
        def _():
            merge_pair(m - 2)

            @pl.when(m - 2 >= SUBS)
            def _():
                start_owner(m - 2)

        nxt = jnp.minimum(m + 1, LAST)
        scores(m, 1, s_b, m_b)
        mix(m, 0, s_a, m_a)
        scores(nxt, 0, s_a, m_a)
        mix(m, 1, s_b, m_b)
        return 0

    lax.fori_loop(0, LAST + 1, step, 0)

    start_pair(LAST)
    merge_pair(LAST - 1)
    start_owner(LAST - 1)
    merge_pair(LAST)
    start_owner(LAST)

    load_w.wait()
    early, late = (0, 1, 2, 3), (4, 5, 6, 7)

    def pairs_in(u, ks):
        for k in ks:
            a_wait_pair(u, k)

    a_handle(0, 6)
    a_handle(0, 7)
    pairs_in(0, early)
    project(0, early)
    a_handle(0, 5)
    finish(1)
    pairs_in(0, late)
    project(0, late)
    y_first(0)
    a_handle(1, 1)
    a_handle(1, 2)
    a_handle(1, 3)
    y_second(0)
    pairs_in(1, early)
    project(1, early)
    a_handle(1, 4)
    z_start(0)
    a_handle(1, 6)
    a_handle(1, 7)
    emit(0)
    a_handle(1, 5)
    pairs_in(1, late)
    project(1, late)
    y_first(1)
    y_second(1)
    z_start(1)
    emit(1)

    for u in range(SUBS):
        q_drain(u)
        a_drain(u)
        z_copy(u).wait_send()
        for zp in range(2):
            for copy in y1_copies(u, zp) + y2_copies(u, zp):
                copy.wait_send()

    def drain(m, _):
        for copy in pair_send(m):
            copy.wait_send()

        @pl.when(m >= SUBS)
        def _():
            for copy in owner_send(m):
                copy.wait_send()

        return 0

    lax.fori_loop(0, LAST + 1, drain, 0)


def shards(queries, cache_keys, cache_values, bounds, out_weight, residual):
    rows, cols = queries.shape
    prompts, span, hd = cache_keys.shape
    out_rows, width = residual.shape
    hr = rows // SUBS
    vmem = pl.BlockSpec(memory_space=pltpu.VMEM)
    hbm = pl.BlockSpec(memory_space=pl.ANY)
    n = SUBS * CHIPS
    unit = GROUPS * hr
    dma = lambda *s: pltpu.SemaphoreType.DMA(s)
    gather_sems = [
        dma(SUBS, 4), dma(SUBS, CHIPS), dma(SUBS, 2), dma(SUBS, 4), dma(SUBS, CHIPS, 2), dma(SUBS, 2, 2),
    ]
    return pl.pallas_call(
        kernel,
        out_shape=jax.ShapeDtypeStruct(residual.shape, BF16),
        in_specs=[pl.BlockSpec(memory_space=pltpu.SMEM), vmem, hbm, hbm, hbm, vmem],
        out_specs=vmem,
        scratch_shapes=[
            pltpu.VMEM((SUBS, CHIPS, 2, hr, cols), BF16),
            pltpu.VMEM((prompts, span, hd), BF16),
            pltpu.VMEM((prompts, span, 2 * hd), BF16),
            pltpu.VMEM(out_weight.shape, BF16),
            pltpu.VMEM((unit, span), F32),
            pltpu.VMEM((unit, span), F32),
            pltpu.VMEM((unit, hd), F32),
            pltpu.VMEM((unit, hd), F32),
            pltpu.VMEM((n, 2, hr, cols), BF16),
            pltpu.VMEM((n, 2, hr, hd), F32),
            pltpu.VMEM((n, hr, cols), BF16),
            pltpu.VMEM((n, hr, hd), F32),
            pltpu.VMEM((n, hr, cols), BF16),
            pltpu.VMEM((n, hr, hd), F32),
            pltpu.VMEM((n, hr, cols), BF16),
            pltpu.VMEM((n, hr, hd), F32),
            pltpu.VMEM((SUBS, CHIPS, 2, hr, cols), BF16),
            pltpu.VMEM((SUBS, 2, 4, 2, hr, width), BF16),
            pltpu.VMEM((SUBS, 2, hr, width), BF16),
            pltpu.VMEM((SUBS, 2, hr, width), BF16),
            pltpu.VMEM((SUBS, 2, 2, hr, width), BF16),
            pltpu.VMEM((SUBS, 2, 2, hr, width), BF16),
            pltpu.VMEM((SUBS, 2, hr, width), BF16),
            pltpu.VMEM((SUBS, 2, hr, width), BF16),
            dma(3), *gather_sems, *gather_sems,
            dma(n), dma(n), dma(n), dma(n),
            dma(n), dma(n), dma(n), dma(n),
            dma(SUBS, 2, 2), dma(SUBS, 2, 2), dma(SUBS, 2, 2), dma(SUBS, 2, 2), dma(SUBS), dma(SUBS),
        ],
        compiler_params=pltpu.CompilerParams(
            collective_id=0, has_side_effects=True, vmem_limit_bytes=62 * 1024 * 1024
        ),
    )(bounds, queries, cache_keys, cache_values, out_weight, residual)


def solution(mesh):
    in_specs = (
        P("ctx", "heads"),
        P(None, "ctx", "heads"),
        P(None, "ctx", "heads"),
        P(),
        P("heads", "ctx"),
        P("heads", "ctx"),
    )
    out_specs = P("heads", "ctx")
    return jax.shard_map(shards, mesh=mesh, in_specs=in_specs, out_specs=out_specs, check_vma=False)
```

time: 582 us -> 117 us (0.20)
  waiting for transfers between devices: 277 us -> 0 us
  Pallas kernels: 0 us -> 114 us
  other arithmetic: 97.3 us -> 0 us
  matrix products: 89.2 us -> 0 us
  local copies, waits for them, and re-layouts: 83.9 us -> 1.67 us
  between operations: 13.4 us -> 0.01 us
  starting transfers between devices: 10.3 us -> 0 us
  loops' own time: 8.94 us -> 0 us
    ppermute x64 -> x0, waiting for transfers between devices: 163 us -> none  [shifted(): return lax.ppermute(block, axis, route)]
    pallas_call x0 -> x1, Pallas kernels: none -> 114 us  [shards(): pl.pallas_call(kernel, out_shape=jax.ShapeDtypeStruct(residual.shape, BF1...]
    dot_general x129 -> x0, matrix products: 89.2 us -> none  [the longest x64 46.1 us: one_block(): jnp.einsum('rkgj,jkd->rkgd', weights.astype(jnp.bfloat16), value_block, p...]
    reduce_scatter x1 -> x0, waiting for transfers between devices: 76.9 us -> none  [shards(): lax.psum_scatter(partial_rows.astype(jnp.bfloat16), 'heads', scatter_dime...]
    reduce_sum x64 -> x0, other arithmetic: 44.4 us -> none  [one_block(): weight_sum = weight_sum * keeping + jnp.sum(weights, axis=3)]
    lt x64 -> x0, other arithmetic: 40.9 us -> none  [one_block(): key_pos[None, :] < limits[1]]
    slice x64 -> x0, local copies, waits for them, and re-layouts: 38.7 us -> none  [one_block(): limits[1]]
    all_gather x1 -> x0, waiting for transfers between devices: 37.2 us -> none  [shards(): lax.all_gather(attended, 'ctx', axis=0, tiled=True)]
  transfers between devices with their start and end apart: 66 -> 0, of which waited for: 18 -> 0; matrix products, arithmetic and copies ran while one was open for 0% -> 0% of each run, Pallas kernels for 0% -> 0%
where the time goes in v2:
time: 117 us; the launch traced here: 116 us
  Pallas kernels  114 us (97%)
  local copies, waits for them, and re-layouts  1.67 us (1%)
    pallas_call x1, Pallas kernels, shards(): pl.pallas_call(kernel, out_shape=jax.ShapeDtypeStruct(residual.shape, BF1...  114 us

profile of v2, /device:TPU:0, one launch (start us, length us, event | category | flops | bytes accessed | tf_op | source)
XLA Modules:
  0.0 115.7 jit_solution(11807335741025194844)
XLA Ops:
  0.0 114.0 %shard_map.64 = bf16[128,1024]{1,0:T(8,128)(2,1)} custom-call(s32[2,2]{1,0:T(2,128)} %bounds.1, bf16[64,2048]{1,0:T(8,128)(2,1)} %q_ref.1, bf16[2,2048,128]{2,1,0:T(8,128)(2,1)} %k_hbm.1, bf16[2,2048,128]{2,1,0:T(8,128)(2,1)} %v_hbm.1, bf16[2048,1024]{1,0:T(8,128)(2,1)} %w_hbm.1, bf16[128,1024]{1,0:T(8,128)(2,1)} %res_ref.1), custom_call_target="tpu_custom_call" | custom-call | tf_op jit(solution)/shard_map/pallas_call | solution.py:466
  114.0 1.7 %copy.8 = bf16[128,1024]{1,0:T(8,128)(2,1)} copy(bf16[128,1024]{1,0:T(8,128)(2,1)} %shard_map.64) | data formatting | bytes 524288

commit v3 on v2

--- a/solution.py
+++ b/solution.py
@@ -22,6 +22,11 @@
 F32 = jnp.float32
 MESH = pl.DeviceIdType.MESH
 OFFSETS = ((0, 0), (0, 1), (1, 0), (3, 0), (2, 0), (2, 1), (1, 1), (3, 1))
+STEPS = tuple(
+    [(0, 0), (1, 0)]
+    + [(0, k) for k in (1, 2, 3, 4, 5, 6, 7)]
+    + [(1, k) for k in (4, 6, 5, 7, 1, 2, 3)]
+)
 
 
 def pick(k, values):
@@ -38,31 +43,34 @@
 
 
 def sub_and_pair(m):
-    rest = m - SUBS
-    if isinstance(m, int):
-        return (m, 0) if m < SUBS else (rest // (CHIPS - 1), rest % (CHIPS - 1) + 1)
-    own = m < SUBS
-    rest = jnp.maximum(rest, 0)
-    return (
-        jnp.where(own, m, rest // (CHIPS - 1)),
-        jnp.where(own, 0, rest % (CHIPS - 1) + 1),
-    )
+    return pick(m, [u for u, _ in STEPS]), pick(m, [k for _, k in STEPS])
 
 
 def step_of(u, k):
-    return u if k == 0 else SUBS + (CHIPS - 1) * u + k - 1
+    return STEPS.index((u, k))
+
+
+def unit_of(m, i):
+    if isinstance(m, int) and m < SUBS:
+        return i, 0, m
+    return *sub_and_pair(m), i
+
+
+def slot_of(m, i):
+    return (i, m) if isinstance(m, int) and m < SUBS else (m, i)
 
 
 def kernel(
     bounds, q_ref, k_hbm, v_hbm, w_hbm, res_ref, out_ref,
     q_all, k_buf, v_buf, w_buf, s_a, s_b, m_a, m_b,
-    o_all, lse_all, rc, rc_lse, mx, mx_lse, rx, rx_lse,
-    att, pp, yl, yr, ra, rb, zs, rz,
+    o_all, lse_all, rc, rc_lse, mx, mx_lse, rx, rx_lse, xr, xr_lse,
+    att, pp, yl, yr, ra, rb, zs, zr, rz,
     local_sem, *sems,
 ):
     q_sems, a_sems, (c_send, c_recv, cl_send, cl_recv), (x_send, x_recv, xl_send, xl_recv), (
-        y1_send, y1_recv, y2_send, y2_recv, z_send, z_recv,
-    ) = sems[:6], sems[6:12], sems[12:16], sems[16:20], sems[20:]
+        y1_send, y1_recv, y2_send, y2_recv, z1_send, z1_recv, z2_send, z2_recv,
+        h1_send, h1_recv, h2_send, h2_recv,
+    ) = sems[:5], sems[5:10], sems[10:14], sems[14:18], sems[18:]
     me = lax.axis_index("ctx")
     hd = lax.axis_index("heads")
     x, zl, c = me // 4, (me // 2) % 2, me % 2
@@ -81,7 +89,9 @@
     left = ctx_at(3, 0, 0)
     up = zh * 4 + (y + 1) % 4
     down = zh * 4 + (y + 3) % 4
-    across = (1 - zh) * 4 + y
+    above = ((zh + zl) % 2) * 4 + y
+    below = ((zh + 1 - zl) % 2) * 4 + y
+    other = (1 - zh) * 4 + y
 
     def remote(src, dst, send, recv, **where):
         return pltpu.make_async_remote_copy(
@@ -101,16 +111,16 @@
     for k in range(1, CHIPS):
         dx, dz = offset(k)
         pl.semaphore_signal(barrier, inc=1, device_id={"ctx": ctx_at(dx, dz, 0)}, device_id_type=MESH)
-    for to in (up, down, across):
+    for to in (up, down):
         pl.semaphore_signal(barrier, inc=1, device_id={"heads": to}, device_id_type=MESH)
+    pl.semaphore_signal(barrier, inc=1, device_id={"ctx": zpart, "heads": other}, device_id_type=MESH)
     for u in range(SUBS):
         q_all[u, 0, 0] = q_ref[pl.ds(u * hr, hr), :]
     for p in range(2):
         v_buf[p, :, pl.ds(HD, HD)] = jnp.ones((span, HD), BF16)
-    pl.semaphore_wait(barrier, 1 + (CHIPS - 1) + 3)
 
     def gather(buf, sems, own):
-        s0, sc, sz, sh, rv, rh = sems
+        s0, sc, sh, rv, rh = sems
 
         def whole(u, k, dc, send, to, src=None):
             return remote(buf.at[u, k, dc] if src is None else src, buf.at[u, k, dc], send, rv.at[u, k, dc], ctx=to)
@@ -119,6 +129,8 @@
             i = 0 if top else 1
             rows = pl.ds(i * hh, hh)
             return remote(buf.at[u, src_k, 0, rows], buf.at[u, k, 0, rows], send, rh.at[u, k - 4, i], ctx=to)
+
+        top, bottom = True, False
 
         def stage(u, k):
             if k == 0:
@@ -131,21 +143,24 @@
                 ]
             here = buf.at[u, k, 0]
             out = []
+            if k == 1:
+                out.append(part(u, 7, bottom, 1, sh.at[u, 4], right))
+                out.append(part(u, 6, bottom, 1, sh.at[u, 5], left))
             if k == 2:
-                out.append(part(u, 4, False, 2, sh.at[u, 0], left))
-                out.append(whole(u, 6, 0, sz.at[u, 0], zpart, here))
+                out.append(part(u, 6, top, 2, sh.at[u, 6], zpart))
+                out.append(part(u, 4, bottom, 2, sh.at[u, 0], left))
             if k == 3:
-                out.append(part(u, 4, True, 3, sh.at[u, 1], right))
-                out.append(whole(u, 7, 0, sz.at[u, 1], zpart, here))
+                out.append(part(u, 7, top, 3, sh.at[u, 7], zpart))
+                out.append(part(u, 4, top, 3, sh.at[u, 1], right))
             if k == 6:
-                out.append(part(u, 5, False, 6, sh.at[u, 2], left))
+                out.append(part(u, 5, bottom, 6, sh.at[u, 2], left))
             if k == 7:
-                out.append(part(u, 5, True, 7, sh.at[u, 3], right))
+                out.append(part(u, 5, top, 7, sh.at[u, 3], right))
             out.append(whole(u, k, 1, sc.at[u, k], partner, here))
             return out
 
         def arrive(u, k):
-            if k in (4, 5):
+            if k >= 4:
                 part(u, k, True, k, sh.at[u, 0], right).wait_recv()
                 part(u, k, False, k, sh.at[u, 0], left).wait_recv()
             else:
@@ -170,25 +185,18 @@
     q_handle, q_wait_pair, q_drain, q_stage = gather(q_all, q_sems, lambda u: q_ref.at[pl.ds(u * hr, hr)])
     a_handle, a_wait_pair, a_drain, _ = gather(att, a_sems, lambda u: att.at[u, 0, 0])
 
-    q_handle(0, 0)
-    for u in range(1, SUBS):
-        q_stage(u, 0)[0].start()
-
     def q_rest(u):
         for copy in q_stage(u, 0)[1:]:
             copy.start()
 
-    load_k.wait()
-
-    def place(m, dc):
-        u, k = sub_and_pair(m)
+    def place(u, k, dc):
         dx, dz = offset(k)
         t = ctx_at(dx, dz, dc)
         return t // 8, (t % 8) * (hr * SUBS) + u * hr
 
-    def scores(m, dc, s_ref, m_ref):
-        u, k = sub_and_pair(m)
-        p, within = place(m, dc)
+    def scores(m, i, s_ref, m_ref):
+        u, k, dc = unit_of(m, i)
+        p, within = place(u, k, dc)
         block = jnp.concatenate(
             [q_all[u, k, dc, :, pl.ds(j * HD, HD)] for j in range(GROUPS)], axis=0
         )
@@ -203,8 +211,10 @@
         s_ref[...] = s
         m_ref[...] = jnp.broadcast_to(jnp.max(s, axis=1, keepdims=True), (unit, HD))
 
-    def mix(m, dc, s_ref, m_ref):
-        p, _ = place(m, dc)
+    def mix(m, i, s_ref, m_ref):
+        u, k, dc = unit_of(m, i)
+        p, _ = place(u, k, dc)
+        to, core = slot_of(m, i)
         top = m_ref[...]
         weights = jnp.exp2((s_ref[...] - jnp.concatenate([top] * (span // HD), axis=1)) * SCALE2)
         both = jnp.dot(weights.astype(BF16), v_buf[p], preferred_element_type=F32)
@@ -215,10 +225,10 @@
         t_c = jnp.ones((hr, HD), F32)
         for h in range(GROUPS):
             part = slice(h * hr, (h + 1) * hr)
-            o_all[m, dc, :, pl.ds(h * HD, HD)] = mixed[part]
+            o_all[to, core, :, pl.ds(h * HD, HD)] = mixed[part]
             m_c = jnp.where(lane == h, top[part], m_c)
             t_c = jnp.where(lane == h, total[part], t_c)
-        lse_all[m, dc] = m_c * SCALE2 + jnp.log(t_c) * LOG2E
+        lse_all[to, core] = m_c * SCALE2 + jnp.log(t_c) * LOG2E
 
     def merge(parts, out, out_lse):
         lses = [lse[...] for _, lse in parts]
@@ -252,6 +262,31 @@
             remote(mx_lse.at[m], rx_lse.at[m], xl_send.at[m], xl_recv.at[m], ctx=to),
         )
 
+    def half_copies(u, k, forward):
+        m, d, dz = step_of(u, k), 2 * u + k - 4, OFFSETS[k][1]
+        out = []
+        for i in range(2):
+            rows = pl.ds(i * hh, hh)
+            if forward:
+                to = ctx_at((1, 3)[i], dz, 0)
+                out.append(remote(xr.at[d, rows], rx.at[m, rows], h2_send.at[d, i, 0], h2_recv.at[d, i, 0], ctx=to))
+                out.append(remote(xr_lse.at[d, rows], rx_lse.at[m, rows], h2_send.at[d, i, 1], h2_recv.at[d, i, 1], ctx=to))
+            else:
+                to = (right, left)[i]
+                out.append(remote(mx.at[m, rows], xr.at[d, rows], h1_send.at[d, i, 0], h1_recv.at[d, i, 0], ctx=to))
+                out.append(remote(mx_lse.at[m, rows], xr_lse.at[d, rows], h1_send.at[d, i, 1], h1_recv.at[d, i, 1], ctx=to))
+        return out
+
+    def half_start(u, k):
+        for copy in half_copies(u, k, False):
+            copy.start()
+
+    def half_forward(u, k):
+        for copy in half_copies(u, k, False):
+            copy.wait_recv()
+        for copy in half_copies(u, k, True):
+            copy.start()
+
     def start_pair(m):
         for copy in pair_send(m):
             copy.start()
@@ -269,11 +304,13 @@
             copy.start()
 
     def finish(u):
+        for copy in pair_send(u):
+            copy.wait_recv()
         for k in range(1, CHIPS):
-            for copy in owner_send(step_of(u, k)):
+            for copy in half_copies(u, k, True) if k in (4, 5) else owner_send(step_of(u, k)):
                 copy.wait_recv()
         merge(
-            [(mx.at[step_of(u, 0)], mx_lse.at[step_of(u, 0)])]
+            [(o_all.at[u, 0], lse_all.at[u, 0]), (rc.at[u], rc_lse.at[u])]
             + [(rx.at[step_of(u, k)], rx_lse.at[step_of(u, k)]) for k in range(1, CHIPS)],
             att.at[u, 0, 0], None,
         )
@@ -319,8 +356,20 @@
                 pp[u, zp, yy, i] = (pp[u, zp, yy, i].astype(F32) + got[u, zp].astype(F32)).astype(BF16)
                 second.start()
 
-    def z_copy(u):
-        return remote(zs.at[u], rz.at[u], z_send.at[u], z_recv.at[u], heads=across)
+    def z_copies(u, forward):
+        out = []
+        for i in range(2):
+            to = (above, below)[i]
+            if forward:
+                out.append(remote(zr.at[u, i], rz.at[u, i], z2_send.at[u, i], z2_recv.at[u, i], ctx=zpart, heads=to))
+            else:
+                out.append(remote(zs.at[u, i], zr.at[u, i], z1_send.at[u, i], z1_recv.at[u, i], ctx=zpart, heads=to))
+        return out
+
+    def z_relay(u):
+        for first, second in zip(z_copies(u, False), z_copies(u, True)):
+            first.wait_recv()
+            second.start()
 
     def y_total(u, zp):
         for copy in y2_copies(u, zp):
@@ -329,55 +378,81 @@
 
     def z_start(u):
         zs[u] = y_total(u, far).astype(BF16)
-        z_copy(u).start()
+        for copy in z_copies(u, False):
+            copy.start()
 
     def emit(u):
         total = y_total(u, zh)
-        z_copy(u).wait_recv()
+        for copy in z_copies(u, True):
+            copy.wait_recv()
         total = total + rz[u].astype(F32)
         for cc in range(2):
             rows = pl.ds(cc * hr * SUBS + u * hr, hr)
             out_ref[rows, :] = (res_ref[rows, :].astype(F32) + total[cc]).astype(BF16)
 
+    load_k.wait()
     scores(0, 0, s_a, m_a)
     load_v.wait()
+    scores(0, 1, s_b, m_b)
+    mix(0, 0, s_a, m_a)
+    pl.semaphore_wait(barrier, 1 + (CHIPS - 1) + 3)
+    q_handle(0, 0)
+    q_stage(1, 0)[0].start()
+    mix(0, 1, s_b, m_b)
+    q_wait_pair(0, 0)
+    scores(1, 0, s_a, m_a)
+    q_wait_pair(1, 0)
+    scores(1, 1, s_b, m_b)
+    mix(1, 0, s_a, m_a)
+    for k in (1, 2, 3):
+        q_handle(0, k)
+    scores(2, 0, s_a, m_a)
+    mix(1, 1, s_b, m_b)
+    start_pair(0)
 
     events = {
-        1: [lambda: q_handle(0, 1), lambda: q_handle(0, 2), lambda: q_handle(0, 3)],
-        3: [lambda: q_handle(0, 4), lambda: q_rest(1)],
-        4: [lambda: q_handle(0, 6), lambda: q_handle(0, 7)],
-        5: [lambda: q_handle(0, 5)],
-        6: [lambda: q_handle(1, 1), lambda: q_handle(1, 2), lambda: q_handle(1, 3)],
-        8: [lambda: q_handle(1, 4)],
-        9: [lambda: q_handle(1, 6), lambda: q_handle(1, 7)],
-        11: [lambda: q_handle(1, 5)],
+        3: [lambda: q_handle(0, 4), lambda: q_handle(0, 6), lambda: q_handle(0, 7), lambda: q_rest(1)],
+        5: [lambda: q_handle(0, 5), lambda: q_handle(1, 1), lambda: q_handle(1, 2), lambda: q_handle(1, 3)],
+        7: [lambda: q_handle(1, 4), lambda: q_handle(1, 6), lambda: q_handle(1, 7)],
+        9: [lambda: q_handle(1, 5), lambda: half_forward(0, 4)],
+        10: [lambda: half_forward(0, 5)],
         12: [lambda: finish(0)],
+        13: [lambda: half_forward(1, 4)],
         14: [lambda: a_handle(0, 1), lambda: a_handle(0, 2), lambda: a_handle(0, 3)],
-        15: [lambda: a_handle(0, 4)],
+        15: [lambda: half_forward(1, 5)],
     }
 
     def step(m, _):
-        for at, acts in events.items():
-            @pl.when(m == at)
+        for parity in range(2):
+            @pl.when(m % 2 == parity)
             def _():
-                for act in acts:
-                    act()
-
-        u, k = sub_and_pair(m)
-        q_wait_pair(u, k)
-
-        @pl.when(m >= 1)
-        def _():
-            start_pair(m - 1)
-
-        @pl.when(m >= 2)
+                for at, acts in events.items():
+                    if at % 2 == parity:
+                        @pl.when(m == at)
+                        def _():
+                            for act in acts:
+                                act()
+
+        start_pair(m - 1)
+
+        @pl.when(m >= SUBS + 2)
         def _():
             merge_pair(m - 2)
-
-            @pl.when(m - 2 >= SUBS)
+            far_pair = offset(sub_and_pair(m - 2)[1])[0] == 2
+
+            @pl.when(jnp.logical_not(far_pair))
             def _():
                 start_owner(m - 2)
 
+            @pl.when(far_pair)
+            def _():
+                for u in range(SUBS):
+                    for k in (4, 5):
+                        @pl.when(m - 2 == step_of(u, k))
+                        def _():
+                            half_start(u, k)
+
+        q_wait_pair(*sub_and_pair(m))
         nxt = jnp.minimum(m + 1, LAST)
         scores(m, 1, s_b, m_b)
         mix(m, 0, s_a, m_a)
@@ -385,69 +460,78 @@
         mix(m, 1, s_b, m_b)
         return 0
 
-    lax.fori_loop(0, LAST + 1, step, 0)
+    lax.fori_loop(SUBS, LAST + 1, step, 0)
+
+    early, late = (0, 1, 2, 3), (4, 6, 7, 5)
+
+    def pairs_in(u, ks):
+        for k in ks:
+            a_wait_pair(u, k)
 
     start_pair(LAST)
     merge_pair(LAST - 1)
     start_owner(LAST - 1)
+    load_w.wait()
+    pairs_in(0, early)
+    project(0, early)
     merge_pair(LAST)
     start_owner(LAST)
-
-    load_w.wait()
-    early, late = (0, 1, 2, 3), (4, 5, 6, 7)
-
-    def pairs_in(u, ks):
-        for k in ks:
-            a_wait_pair(u, k)
-
+    a_handle(0, 4)
     a_handle(0, 6)
     a_handle(0, 7)
-    pairs_in(0, early)
-    project(0, early)
+    q_drain(0)
+    finish(1)
     a_handle(0, 5)
-    finish(1)
+    q_drain(1)
     pairs_in(0, late)
     project(0, late)
     y_first(0)
     a_handle(1, 1)
     a_handle(1, 2)
     a_handle(1, 3)
-    y_second(0)
     pairs_in(1, early)
     project(1, early)
+    y_second(0)
     a_handle(1, 4)
-    z_start(0)
     a_handle(1, 6)
     a_handle(1, 7)
-    emit(0)
+    a_drain(0)
     a_handle(1, 5)
     pairs_in(1, late)
     project(1, late)
     y_first(1)
+    z_start(0)
+
+    def drain(m, _):
+        for copy in pair_send(m):
+            copy.wait_send()
+
+        @pl.when((m >= SUBS) & (offset(sub_and_pair(m)[1])[0] != 2))
+        def _():
+            for copy in owner_send(m):
+                copy.wait_send()
+
+        return 0
+
     y_second(1)
+    z_relay(0)
+    lax.fori_loop(0, LAST + 1, drain, 0)
     z_start(1)
+    emit(0)
+    z_relay(1)
+    a_drain(1)
+    for u in range(SUBS):
+        for k in (4, 5):
+            for copy in half_copies(u, k, False) + half_copies(u, k, True):
+                copy.wait_send()
     emit(1)
 
     for u in range(SUBS):
-        q_drain(u)
-        a_drain(u)
-        z_copy(u).wait_send()
+        for copy in z_copies(u, False) + z_copies(u, True):
+            copy.wait_send()
         for zp in range(2):
             for copy in y1_copies(u, zp) + y2_copies(u, zp):
                 copy.wait_send()
-
-    def drain(m, _):
-        for copy in pair_send(m):
-            copy.wait_send()
-
-        @pl.when(m >= SUBS)
-        def _():
-            for copy in owner_send(m):
-                copy.wait_send()
-
-        return 0
-
-    lax.fori_loop(0, LAST + 1, drain, 0)
 
 
 def shards(queries, cache_keys, cache_values, bounds, out_weight, residual):
@@ -461,7 +545,7 @@
     unit = GROUPS * hr
     dma = lambda *s: pltpu.SemaphoreType.DMA(s)
     gather_sems = [
-        dma(SUBS, 4), dma(SUBS, CHIPS), dma(SUBS, 2), dma(SUBS, 4), dma(SUBS, CHIPS, 2), dma(SUBS, 2, 2),
+        dma(SUBS, 4), dma(SUBS, CHIPS), dma(SUBS, 8), dma(SUBS, CHIPS, 2), dma(SUBS, 4, 2),
     ]
     return pl.pallas_call(
         kernel,
@@ -485,6 +569,8 @@
             pltpu.VMEM((n, hr, hd), F32),
             pltpu.VMEM((n, hr, cols), BF16),
             pltpu.VMEM((n, hr, hd), F32),
+            pltpu.VMEM((2 * SUBS, hr, cols), BF16),
+            pltpu.VMEM((2 * SUBS, hr, hd), F32),
             pltpu.VMEM((SUBS, CHIPS, 2, hr, cols), BF16),
             pltpu.VMEM((SUBS, 2, 4, 2, hr, width), BF16),
             pltpu.VMEM((SUBS, 2, hr, width), BF16),
@@ -493,10 +579,13 @@
             pltpu.VMEM((SUBS, 2, 2, hr, width), BF16),
             pltpu.VMEM((SUBS, 2, hr, width), BF16),
             pltpu.VMEM((SUBS, 2, hr, width), BF16),
+            pltpu.VMEM((SUBS, 2, hr, width), BF16),
             dma(3), *gather_sems, *gather_sems,
             dma(n), dma(n), dma(n), dma(n),
             dma(n), dma(n), dma(n), dma(n),
-            dma(SUBS, 2, 2), dma(SUBS, 2, 2), dma(SUBS, 2, 2), dma(SUBS, 2, 2), dma(SUBS), dma(SUBS),
+            dma(SUBS, 2, 2), dma(SUBS, 2, 2), dma(SUBS, 2, 2), dma(SUBS, 2, 2),
+            dma(SUBS, 2), dma(SUBS, 2), dma(SUBS, 2), dma(SUBS, 2),
+            dma(2 * SUBS, 2, 2), dma(2 * SUBS, 2, 2), dma(2 * SUBS, 2, 2), dma(2 * SUBS, 2, 2),
         ],
         compiler_params=pltpu.CompilerParams(
             collective_id=0, has_side_effects=True, vmem_limit_bytes=62 * 1024 * 1024

time: 117 us -> 111 us (0.949)
  Pallas kernels: 114 us -> 109 us
    pallas_call x1, Pallas kernels: 114 us -> 109 us  [shards(): pl.pallas_call(kernel, out_shape=jax.ShapeDtypeStruct(residual.shape, BF1...]
where the time goes in v3:
time: 111 us
  Pallas kernels  109 us (98%)
  local copies, waits for them, and re-layouts  1.67 us (2%)
    pallas_call x1, Pallas kernels, shards(): pl.pallas_call(kernel, out_shape=jax.ShapeDtypeStruct(residual.shape, BF1...  109 us

profile of v3, /device:TPU:0, one launch (start us, length us, event | category | flops | bytes accessed | tf_op | source)
XLA Modules:
  0.0 110.6 jit_solution(5527920066011487534)
XLA Ops:
  0.0 109.0 %shard_map.64 = bf16[128,1024]{1,0:T(8,128)(2,1)} custom-call(s32[2,2]{1,0:T(2,128)} %bounds.1, bf16[64,2048]{1,0:T(8,128)(2,1)} %q_ref.1, bf16[2,2048,128]{2,1,0:T(8,128)(2,1)} %k_hbm.1, bf16[2,2048,128]{2,1,0:T(8,128)(2,1)} %v_hbm.1, bf16[2048,1024]{1,0:T(8,128)(2,1)} %w_hbm.1, bf16[128,1024]{1,0:T(8,128)(2,1)} %res_ref.1), custom_call_target="tpu_custom_call" | custom-call | tf_op jit(solution)/shard_map/pallas_call | solution.py:550
  109.0 1.7 %copy.8 = bf16[128,1024]{1,0:T(8,128)(2,1)} copy(bf16[128,1024]{1,0:T(8,128)(2,1)} %shard_map.64) | data formatting | bytes 524288

commit v4 on v3

--- a/solution.py
+++ b/solution.py
@@ -24,8 +24,8 @@
 OFFSETS = ((0, 0), (0, 1), (1, 0), (3, 0), (2, 0), (2, 1), (1, 1), (3, 1))
 STEPS = tuple(
     [(0, 0), (1, 0)]
-    + [(0, k) for k in (1, 2, 3, 4, 5, 6, 7)]
-    + [(1, k) for k in (4, 6, 5, 7, 1, 2, 3)]
+    + [(0, k) for k in (1, 2, 6, 7, 5, 4, 3)]
+    + [(1, k) for k in (5, 6, 7, 4, 1, 2, 3)]
 )
 
 
@@ -61,15 +61,16 @@
 
 
 def kernel(
-    bounds, q_ref, k_hbm, v_hbm, w_hbm, res_ref, out_ref,
+    bounds, q_ref, k_hbm, v_hbm, w_hbm, res_ref, out_hbm,
     q_all, k_buf, v_buf, w_buf, s_a, s_b, m_a, m_b,
     o_all, lse_all, rc, rc_lse, mx, mx_lse, rx, rx_lse, xr, xr_lse,
+    mz, mz_lse, rm, rm_lse,
     att, pp, yl, yr, ra, rb, zs, zr, rz,
-    local_sem, *sems,
+    out_ref, local_sem, out_sem, *sems,
 ):
     q_sems, a_sems, (c_send, c_recv, cl_send, cl_recv), (x_send, x_recv, xl_send, xl_recv), (
         y1_send, y1_recv, y2_send, y2_recv, z1_send, z1_recv, z2_send, z2_recv,
-        h1_send, h1_recv, h2_send, h2_recv,
+        h1_send, h1_recv, m_send, m_recv,
     ) = sems[:5], sems[5:10], sems[10:14], sems[14:18], sems[18:]
     me = lax.axis_index("ctx")
     hd = lax.axis_index("heads")
@@ -136,10 +137,10 @@
             if k == 0:
                 src = own(u)
                 return [
-                    whole(u, 0, 1, s0.at[u, 0], partner, src),
                     whole(u, 1, 0, s0.at[u, 1], zpart, src),
                     whole(u, 3, 0, s0.at[u, 2], right, src),
                     whole(u, 2, 0, s0.at[u, 3], left, src),
+                    whole(u, 0, 1, s0.at[u, 0], partner, src),
                 ]
             here = buf.at[u, k, 0]
             out = []
@@ -167,10 +168,17 @@
                 whole(u, k, 0, s0.at[u, 0], partner).wait_recv()
 
         def handle(u, k):
+            links(u, k)
+            core(u, k)
+
+        def links(u, k):
             if k:
                 arrive(u, k)
-            for copy in stage(u, k):
+            for copy in stage(u, k)[:-1]:
                 copy.start()
+
+        def core(u, k):
+            stage(u, k)[-1].start()
 
         def wait_pair(u, k):
             whole(u, k, 1, s0.at[0, 0], partner).wait_recv()
@@ -180,14 +188,10 @@
                 for copy in stage(u, k):
                     copy.wait_send()
 
-        return handle, wait_pair, drain, stage
-
-    q_handle, q_wait_pair, q_drain, q_stage = gather(q_all, q_sems, lambda u: q_ref.at[pl.ds(u * hr, hr)])
-    a_handle, a_wait_pair, a_drain, _ = gather(att, a_sems, lambda u: att.at[u, 0, 0])
-
-    def q_rest(u):
-        for copy in q_stage(u, 0)[1:]:
-            copy.start()
+        return handle, wait_pair, drain, links, core
+
+    q_handle, q_wait_pair, q_drain, q_rest, q_core = gather(q_all, q_sems, lambda u: q_ref.at[pl.ds(u * hr, hr)])
+    a_handle, a_wait_pair, a_drain, a_links, a_core = gather(att, a_sems, lambda u: att.at[u, 0, 0])
 
     def place(u, k, dc):
         dx, dz = offset(k)
@@ -232,6 +236,7 @@
 
     def merge(parts, out, out_lse):
         lses = [lse[...] for _, lse in parts]
+        count = lses[0].shape[0]
         top = functools.reduce(jnp.maximum, lses)
         es = [jnp.exp2(lse - top) for lse in lses]
         tot = functools.reduce(lambda a, b: a + b, es)
@@ -243,7 +248,7 @@
             cols = pl.ds(h * HD, HD)
             acc = None
             for (o, _), w in zip(parts, ws):
-                term = o[:, cols].astype(F32) * jnp.broadcast_to(w[:, h:h + 1], (hr, HD))
+                term = o[:, cols].astype(F32) * jnp.broadcast_to(w[:, h:h + 1], (count, HD))
                 acc = term if acc is None else acc + term
             out[:, cols] = acc.astype(BF16)
 
@@ -255,37 +260,37 @@
 
     def owner_send(m):
         _, k = sub_and_pair(m)
-        dx, dz = offset(k)
-        to = ctx_at(dx, dz, 0)
+        dx, _ = offset(k)
+        to = ctx_at(dx, 0, 0)
         return (
             remote(mx.at[m], rx.at[m], x_send.at[m], x_recv.at[m], ctx=to),
             remote(mx_lse.at[m], rx_lse.at[m], xl_send.at[m], xl_recv.at[m], ctx=to),
         )
 
-    def half_copies(u, k, forward):
-        m, d, dz = step_of(u, k), 2 * u + k - 4, OFFSETS[k][1]
+    def half_copies(u, k):
+        m, d = step_of(u, k), 2 * u + k - 4
         out = []
         for i in range(2):
-            rows = pl.ds(i * hh, hh)
-            if forward:
-                to = ctx_at((1, 3)[i], dz, 0)
-                out.append(remote(xr.at[d, rows], rx.at[m, rows], h2_send.at[d, i, 0], h2_recv.at[d, i, 0], ctx=to))
-                out.append(remote(xr_lse.at[d, rows], rx_lse.at[m, rows], h2_send.at[d, i, 1], h2_recv.at[d, i, 1], ctx=to))
-            else:
-                to = (right, left)[i]
-                out.append(remote(mx.at[m, rows], xr.at[d, rows], h1_send.at[d, i, 0], h1_recv.at[d, i, 0], ctx=to))
-                out.append(remote(mx_lse.at[m, rows], xr_lse.at[d, rows], h1_send.at[d, i, 1], h1_recv.at[d, i, 1], ctx=to))
+            rows, to = pl.ds(i * hh, hh), (right, left)[i]
+            out.append(remote(mx.at[m, rows], xr.at[d, rows], h1_send.at[d, i, 0], h1_recv.at[d, i, 0], ctx=to))
+            out.append(remote(mx_lse.at[m, rows], xr_lse.at[d, rows], h1_send.at[d, i, 1], h1_recv.at[d, i, 1], ctx=to))
         return out
 
     def half_start(u, k):
-        for copy in half_copies(u, k, False):
+        for copy in half_copies(u, k):
             copy.start()
 
-    def half_forward(u, k):
-        for copy in half_copies(u, k, False):
+    def absorb(u, k):
+        m, i, via = step_of(u, k), k % 2, 4 + k // 6
+        d = 2 * u + via - 4
+        rows = pl.ds(i * hh, hh)
+        for copy in half_copies(u, via)[2 * i:2 * i + 2]:
             copy.wait_recv()
-        for copy in half_copies(u, k, True):
-            copy.start()
+        merge(
+            [(mx.at[m, rows], mx_lse.at[m, rows]), (xr.at[d, rows], xr_lse.at[d, rows])],
+            mx.at[m, rows], mx_lse.at[m, rows],
+        )
+        start_owner(m)
 
     def start_pair(m):
         for copy in pair_send(m):
@@ -294,6 +299,9 @@
     def merge_pair(m):
         for copy in pair_send(m):
             copy.wait_recv()
+        merge_local(m)
+
+    def merge_local(m):
         merge(
             [(o_all.at[m, 0], lse_all.at[m, 0]), (rc.at[m], rc_lse.at[m])],
             mx.at[m], mx_lse.at[m],
@@ -303,17 +311,33 @@
         for copy in owner_send(m):
             copy.start()
 
+    def received(u, k):
+        for copy in owner_send(step_of(u, k)):
+            copy.wait_recv()
+        m = step_of(u, k)
+        return rx.at[m], rx_lse.at[m]
+
+    def row_copies(u):
+        return (
+            remote(mz.at[u], rm.at[u], m_send.at[u, 0], m_recv.at[u, 0], ctx=zpart),
+            remote(mz_lse.at[u], rm_lse.at[u], m_send.at[u, 1], m_recv.at[u, 1], ctx=zpart),
+        )
+
+    def row_merge(u):
+        own = step_of(u, 1)
+        parts = [(mx.at[own], mx_lse.at[own])] + [received(u, k) for k in (6, 7)]
+        merge(parts, mz.at[u], mz_lse.at[u])
+        for copy in row_copies(u):
+            copy.start()
+
     def finish(u):
         for copy in pair_send(u):
             copy.wait_recv()
-        for k in range(1, CHIPS):
-            for copy in half_copies(u, k, True) if k in (4, 5) else owner_send(step_of(u, k)):
-                copy.wait_recv()
-        merge(
-            [(o_all.at[u, 0], lse_all.at[u, 0]), (rc.at[u], rc_lse.at[u])]
-            + [(rx.at[step_of(u, k)], rx_lse.at[step_of(u, k)]) for k in range(1, CHIPS)],
-            att.at[u, 0, 0], None,
-        )
+        parts = [(o_all.at[u, 0], lse_all.at[u, 0]), (rc.at[u], rc_lse.at[u])]
+        parts += [received(u, k) for k in (2, 3)]
+        for copy in row_copies(u):
+            copy.wait_recv()
+        merge(parts + [(rm.at[u], rm_lse.at[u])], att.at[u, 0, 0], None)
         a_handle(u, 0)
 
     def project(u, ks):
@@ -389,15 +413,25 @@
         for cc in range(2):
             rows = pl.ds(cc * hr * SUBS + u * hr, hr)
             out_ref[rows, :] = (res_ref[rows, :].astype(F32) + total[cc]).astype(BF16)
+            out_copy(u, cc).start()
+
+    def out_copy(u, cc):
+        rows = pl.ds(cc * hr * SUBS + u * hr, hr)
+        return pltpu.make_async_copy(out_ref.at[rows], out_hbm.at[rows], out_sem.at[u, cc])
 
     load_k.wait()
     scores(0, 0, s_a, m_a)
     load_v.wait()
     scores(0, 1, s_b, m_b)
     mix(0, 0, s_a, m_a)
+    o_all[LAST + 1, 0] = jnp.zeros((hr, GROUPS * HD), BF16)
+    rc[LAST + 1] = jnp.zeros((hr, GROUPS * HD), BF16)
+    lse_all[LAST + 1, 0] = jnp.zeros((hr, HD), F32)
+    rc_lse[LAST + 1] = jnp.zeros((hr, HD), F32)
     pl.semaphore_wait(barrier, 1 + (CHIPS - 1) + 3)
-    q_handle(0, 0)
-    q_stage(1, 0)[0].start()
+    q_core(0, 0)
+    q_rest(0, 0)
+    q_core(1, 0)
     mix(0, 1, s_b, m_b)
     q_wait_pair(0, 0)
     scores(1, 0, s_a, m_a)
@@ -411,15 +445,19 @@
     start_pair(0)
 
     events = {
-        3: [lambda: q_handle(0, 4), lambda: q_handle(0, 6), lambda: q_handle(0, 7), lambda: q_rest(1)],
-        5: [lambda: q_handle(0, 5), lambda: q_handle(1, 1), lambda: q_handle(1, 2), lambda: q_handle(1, 3)],
-        7: [lambda: q_handle(1, 4), lambda: q_handle(1, 6), lambda: q_handle(1, 7)],
-        9: [lambda: q_handle(1, 5), lambda: half_forward(0, 4)],
-        10: [lambda: half_forward(0, 5)],
-        12: [lambda: finish(0)],
-        13: [lambda: half_forward(1, 4)],
-        14: [lambda: a_handle(0, 1), lambda: a_handle(0, 2), lambda: a_handle(0, 3)],
-        15: [lambda: half_forward(1, 5)],
+        2: [lambda: q_rest(1, 0)],
+        3: [lambda: q_handle(0, 6), lambda: q_handle(0, 7), lambda: q_handle(0, 4)],
+        4: [lambda: q_handle(1, 1), lambda: q_handle(1, 2), lambda: q_handle(1, 3)],
+        5: [lambda: q_handle(0, 5)],
+        6: [lambda: q_handle(1, 6), lambda: q_handle(1, 7), lambda: q_handle(1, 4)],
+        8: [lambda: q_handle(1, 5)],
+        9: [lambda: half_start(0, 5)],
+        10: [lambda: half_start(0, 4)],
+        11: [lambda: absorb(0, 6), lambda: absorb(0, 7)],
+        12: [lambda: half_start(1, 5), lambda: absorb(0, 2), lambda: absorb(0, 3)],
+        13: [lambda: row_merge(0)],
+        14: [lambda: absorb(1, 6), lambda: absorb(1, 7)],
+        15: [lambda: half_start(1, 4), lambda: finish(0)],
     }
 
     def step(m, _):
@@ -437,20 +475,8 @@
 
         @pl.when(m >= SUBS + 2)
         def _():
-            merge_pair(m - 2)
-            far_pair = offset(sub_and_pair(m - 2)[1])[0] == 2
-
-            @pl.when(jnp.logical_not(far_pair))
-            def _():
-                start_owner(m - 2)
-
-            @pl.when(far_pair)
-            def _():
-                for u in range(SUBS):
-                    for k in (4, 5):
-                        @pl.when(m - 2 == step_of(u, k))
-                        def _():
-                            half_start(u, k)
+            for copy in pair_send(m - 2):
+                copy.wait_recv()
 
         q_wait_pair(*sub_and_pair(m))
         nxt = jnp.minimum(m + 1, LAST)
@@ -458,6 +484,7 @@
         mix(m, 0, s_a, m_a)
         scores(nxt, 0, s_a, m_a)
         mix(m, 1, s_b, m_b)
+        merge_local(jnp.where(m >= SUBS + 2, m - 2, LAST + 1))
         return 0
 
     lax.fori_loop(SUBS, LAST + 1, step, 0)
@@ -470,33 +497,35 @@
 
     start_pair(LAST)
     merge_pair(LAST - 1)
-    start_owner(LAST - 1)
+    row_merge(1)
+    absorb(1, 2)
+    merge_pair(LAST)
+    absorb(1, 3)
+    for k in (1, 2, 3):
+        a_links(0, k)
+    for k in (1, 2, 3):
+        a_core(0, k)
     load_w.wait()
+    q_drain(0)
+    q_drain(1)
+    finish(1)
+    for k in (6, 7, 4):
+        a_handle(0, k)
     pairs_in(0, early)
     project(0, early)
-    merge_pair(LAST)
-    start_owner(LAST)
-    a_handle(0, 4)
-    a_handle(0, 6)
-    a_handle(0, 7)
-    q_drain(0)
-    finish(1)
+    for k in (1, 2, 3):
+        a_handle(1, k)
     a_handle(0, 5)
-    q_drain(1)
     pairs_in(0, late)
     project(0, late)
     y_first(0)
-    a_handle(1, 1)
-    a_handle(1, 2)
-    a_handle(1, 3)
     pairs_in(1, early)
     project(1, early)
+    for k in (6, 7, 4):
+        a_handle(1, k)
     y_second(0)
-    a_handle(1, 4)
-    a_handle(1, 6)
-    a_handle(1, 7)
+    a_handle(1, 5)
     a_drain(0)
-    a_handle(1, 5)
     pairs_in(1, late)
     project(1, late)
     y_first(1)
@@ -506,7 +535,7 @@
         for copy in pair_send(m):
             copy.wait_send()
 
-        @pl.when((m >= SUBS) & (offset(sub_and_pair(m)[1])[0] != 2))
+        @pl.when((m >= SUBS) & (offset(sub_and_pair(m)[1])[0] % 2 == 1))
         def _():
             for copy in owner_send(m):
                 copy.wait_send()
@@ -522,11 +551,15 @@
     a_drain(1)
     for u in range(SUBS):
         for k in (4, 5):
-            for copy in half_copies(u, k, False) + half_copies(u, k, True):
+            for copy in half_copies(u, k):
                 copy.wait_send()
+        for copy in row_copies(u):
+            copy.wait_send()
     emit(1)
 
     for u in range(SUBS):
+        for cc in range(2):
+            out_copy(u, cc).wait()
         for copy in z_copies(u, False) + z_copies(u, True):
             copy.wait_send()
         for zp in range(2):
@@ -551,7 +584,7 @@
         kernel,
         out_shape=jax.ShapeDtypeStruct(residual.shape, BF16),
         in_specs=[pl.BlockSpec(memory_space=pltpu.SMEM), vmem, hbm, hbm, hbm, vmem],
-        out_specs=vmem,
+        out_specs=hbm,
         scratch_shapes=[
             pltpu.VMEM((SUBS, CHIPS, 2, hr, cols), BF16),
             pltpu.VMEM((prompts, span, hd), BF16),
@@ -561,16 +594,20 @@
             pltpu.VMEM((unit, span), F32),
             pltpu.VMEM((unit, hd), F32),
             pltpu.VMEM((unit, hd), F32),
-            pltpu.VMEM((n, 2, hr, cols), BF16),
-            pltpu.VMEM((n, 2, hr, hd), F32),
-            pltpu.VMEM((n, hr, cols), BF16),
-            pltpu.VMEM((n, hr, hd), F32),
-            pltpu.VMEM((n, hr, cols), BF16),
-            pltpu.VMEM((n, hr, hd), F32),
+            pltpu.VMEM((n + 1, 2, hr, cols), BF16),
+            pltpu.VMEM((n + 1, 2, hr, hd), F32),
+            pltpu.VMEM((n + 1, hr, cols), BF16),
+            pltpu.VMEM((n + 1, hr, hd), F32),
+            pltpu.VMEM((n + 1, hr, cols), BF16),
+            pltpu.VMEM((n + 1, hr, hd), F32),
             pltpu.VMEM((n, hr, cols), BF16),
             pltpu.VMEM((n, hr, hd), F32),
             pltpu.VMEM((2 * SUBS, hr, cols), BF16),
             pltpu.VMEM((2 * SUBS, hr, hd), F32),
+            pltpu.VMEM((SUBS, hr, cols), BF16),
+            pltpu.VMEM((SUBS, hr, hd), F32),
+            pltpu.VMEM((SUBS, hr, cols), BF16),
+            pltpu.VMEM((SUBS, hr, hd), F32),
             pltpu.VMEM((SUBS, CHIPS, 2, hr, cols), BF16),
             pltpu.VMEM((SUBS, 2, 4, 2, hr, width), BF16),
             pltpu.VMEM((SUBS, 2, hr, width), BF16),
@@ -580,12 +617,14 @@
             pltpu.VMEM((SUBS, 2, hr, width), BF16),
             pltpu.VMEM((SUBS, 2, hr, width), BF16),
             pltpu.VMEM((SUBS, 2, hr, width), BF16),
-            dma(3), *gather_sems, *gather_sems,
+            pltpu.VMEM((out_rows, width), BF16),
+            dma(3), dma(SUBS, 2), *gather_sems, *gather_sems,
             dma(n), dma(n), dma(n), dma(n),
             dma(n), dma(n), dma(n), dma(n),
             dma(SUBS, 2, 2), dma(SUBS, 2, 2), dma(SUBS, 2, 2), dma(SUBS, 2, 2),
             dma(SUBS, 2), dma(SUBS, 2), dma(SUBS, 2), dma(SUBS, 2),
-            dma(2 * SUBS, 2, 2), dma(2 * SUBS, 2, 2), dma(2 * SUBS, 2, 2), dma(2 * SUBS, 2, 2),
+            dma(2 * SUBS, 2, 2), dma(2 * SUBS, 2, 2),
+            dma(SUBS, 2), dma(SUBS, 2),
         ],
         compiler_params=pltpu.CompilerParams(
             collective_id=0, has_side_effects=True, vmem_limit_bytes=62 * 1024 * 1024

time: 111 us -> 109 us (0.982)
  Pallas kernels: 109 us -> 106 us
    pallas_call x1, Pallas kernels: 109 us -> 106 us  [shards(): pl.pallas_call(kernel, out_shape=jax.ShapeDtypeStruct(residual.shape, BF1...]
where the time goes in v4:
time: 109 us; the launch traced here: 108 us
  Pallas kernels  106 us (97%)
  local copies, waits for them, and re-layouts  1.67 us (2%)
    pallas_call x1, Pallas kernels, shards(): pl.pallas_call(kernel, out_shape=jax.ShapeDtypeStruct(residual.shape, BF1...  106 us

profile of v4, /device:TPU:0, one launch (start us, length us, event | category | flops | bytes accessed | tf_op | source)
XLA Modules:
  0.0 107.7 jit_solution(18401546137957241959)
XLA Ops:
  0.0 106.0 %shard_map.64 = bf16[128,1024]{1,0:T(8,128)(2,1)} custom-call(s32[2,2]{1,0:T(2,128)} %bounds.1, bf16[64,2048]{1,0:T(8,128)(2,1)} %q_ref.1, bf16[2,2048,128]{2,1,0:T(8,128)(2,1)} %k_hbm.1, bf16[2,2048,128]{2,1,0:T(8,128)(2,1)} %v_hbm.1, bf16[2048,1024]{1,0:T(8,128)(2,1)} %w_hbm.1, bf16[128,1024]{1,0:T(8,128)(2,1)} %res_ref.1), custom_call_target="tpu_custom_call" | custom-call | tf_op jit(solution)/shard_map/pallas_call | solution.py:583
  106.0 1.7 %copy.8 = bf16[128,1024]{1,0:T(8,128)(2,1)} copy(bf16[128,1024]{1,0:T(8,128)(2,1)} %shard_map.64) | data formatting | bytes 524288

commit v5 on v4

--- a/solution.py
+++ b/solution.py
@@ -452,12 +452,10 @@
         6: [lambda: q_handle(1, 6), lambda: q_handle(1, 7), lambda: q_handle(1, 4)],
         8: [lambda: q_handle(1, 5)],
         9: [lambda: half_start(0, 5)],
-        10: [lambda: half_start(0, 4)],
-        11: [lambda: absorb(0, 6), lambda: absorb(0, 7)],
-        12: [lambda: half_start(1, 5), lambda: absorb(0, 2), lambda: absorb(0, 3)],
-        13: [lambda: row_merge(0)],
-        14: [lambda: absorb(1, 6), lambda: absorb(1, 7)],
-        15: [lambda: half_start(1, 4), lambda: finish(0)],
+        10: [lambda: half_start(0, 4), lambda: absorb(0, 6), lambda: absorb(0, 7)],
+        12: [lambda: half_start(1, 5), lambda: absorb(0, 2), lambda: absorb(0, 3), lambda: row_merge(0)],
+        14: [lambda: absorb(1, 6), lambda: absorb(1, 7), lambda: finish(0)],
+        15: [lambda: half_start(1, 4)],
     }
 
     def step(m, _):
@@ -496,40 +494,42 @@
             a_wait_pair(u, k)
 
     start_pair(LAST)
+    for k in (1, 2, 3):
+        a_links(0, k)
     merge_pair(LAST - 1)
     row_merge(1)
     absorb(1, 2)
     merge_pair(LAST)
     absorb(1, 3)
     for k in (1, 2, 3):
-        a_links(0, k)
-    for k in (1, 2, 3):
         a_core(0, k)
     load_w.wait()
     q_drain(0)
-    q_drain(1)
+    pairs_in(0, early)
+    project(0, early)
     finish(1)
     for k in (6, 7, 4):
         a_handle(0, k)
-    pairs_in(0, early)
-    project(0, early)
-    for k in (1, 2, 3):
-        a_handle(1, k)
+    q_drain(1)
     a_handle(0, 5)
     pairs_in(0, late)
     project(0, late)
     y_first(0)
+    for k in (1, 2, 3):
+        a_handle(1, k)
+    y_second(0)
     pairs_in(1, early)
     project(1, early)
     for k in (6, 7, 4):
         a_handle(1, k)
-    y_second(0)
+    a_drain(0)
     a_handle(1, 5)
-    a_drain(0)
+    z_start(0)
     pairs_in(1, late)
     project(1, late)
     y_first(1)
-    z_start(0)
+    z_relay(0)
+    emit(0)
 
     def drain(m, _):
         for copy in pair_send(m):
@@ -543,10 +543,8 @@
         return 0
 
     y_second(1)
-    z_relay(0)
     lax.fori_loop(0, LAST + 1, drain, 0)
     z_start(1)
-    emit(0)
     z_relay(1)
     a_drain(1)
     for u in range(SUBS):

time: 109 us -> 114 us (1.046)
  Pallas kernels: 106 us -> 112 us
    pallas_call x1, Pallas kernels: 106 us -> 112 us  [shards(): pl.pallas_call(kernel, out_shape=jax.ShapeDtypeStruct(residual.shape, BF1...]
where the time goes in v5:
time: 114 us
  Pallas kernels  112 us (98%)
  local copies, waits for them, and re-layouts  1.67 us (1%)
    pallas_call x1, Pallas kernels, shards(): pl.pallas_call(kernel, out_shape=jax.ShapeDtypeStruct(residual.shape, BF1...  112 us

profile of v5, /device:TPU:0, one launch (start us, length us, event | category | flops | bytes accessed | tf_op | source)
XLA Modules:
  0.0 113.8 jit_solution(10058822600690513994)
XLA Ops:
  0.0 112.1 %shard_map.64 = bf16[128,1024]{1,0:T(8,128)(2,1)} custom-call(s32[2,2]{1,0:T(2,128)} %bounds.1, bf16[64,2048]{1,0:T(8,128)(2,1)} %q_ref.1, bf16[2,2048,128]{2,1,0:T(8,128)(2,1)} %k_hbm.1, bf16[2,2048,128]{2,1,0:T(8,128)(2,1)} %v_hbm.1, bf16[2048,1024]{1,0:T(8,128)(2,1)} %w_hbm.1, bf16[128,1024]{1,0:T(8,128)(2,1)} %res_ref.1), custom_call_target="tpu_custom_call" | custom-call | tf_op jit(solution)/shard_map/pallas_call | solution.py:581
  112.1 1.7 %copy.8 = bf16[128,1024]{1,0:T(8,128)(2,1)} copy(bf16[128,1024]{1,0:T(8,128)(2,1)} %shard_map.64) | data formatting | bytes 524288
